TPU v7x, 512 devices: a whole 4x4x16 slice. The times are simulated.
512 devices in a mesh: delay: 32 (over z, x_hi), src: 8 (over x_lo, y), tgt: 2 (over core).
Axes of the slice: x: 4 (x_hi: 2, x_lo: 2; x = x_hi * 2 + x_lo), y: 4, z: 16, core: 2. Of those that a mesh axis runs over, the one named last changes fastest.
Arguments:
- blocks: bfloat16 [32, 8, 2, 32, 128, 128], P('delay', 'src', 'tgt'), may hold values from -0.0390625 to 0.0390625
- coords: int32 [32, 8, 2, 32, 2], P('delay', 'src', 'tgt'), may hold values from 0 to 31, as said below
- counts: int32 [32, 8, 2], P('delay', 'src', 'tgt'), may hold values from 16 to 32, as said below
- history: bfloat16 [32, 2, 4096, 128], P('delay', None, 'src'), may hold values from -6 to 6
- excitation: bfloat16 [2, 2, 4096, 128], P(None, 'tgt', 'src'), may hold values from -6 to 6
- inverse: bfloat16 [2, 32, 128, 128], P('tgt', 'src'), may hold values from -0.5 to 0.5
Outputs:
- currents: bfloat16 [2, 2, 4096, 128], P(None, 'tgt', 'src')
Inputs may be any that keep to these rules, and one draw needn't show every extreme that they name: `counts`: at most 32 used slots in a tile; in every draw some tile has exactly 32. `coords`: within one tile the 32 slots name distinct (row block, column block) pairs, row blocks below 32 and column blocks below 8; slots at or past the tile's count are not used.
All inputs are finite; a program needn't handle non-finite values.
Results may differ from a plain program's by a relative error of at most 0.017.
Values may be sent and summed in bfloat16 or wider, within the bound.
A program may use at most 64 MiB of HBM per device.

v0:
```python
import jax
import jax.numpy as jnp
from jax import lax
from jax.sharding import PartitionSpec as P


def from_behind(array, axis, by):
    peers = lax.axis_size(axis)
    pairs = [(i, i + by) for i in range(peers) if 0 <= i + by < peers]
    return lax.ppermute(array, axis, pairs)


def shards(blocks, coords, counts, history, excitation, inverse):
    block_edge = blocks.shape[-1]
    slot_count = blocks.shape[3]
    halves = history.shape[1]
    owned_rows = history.shape[2]
    excite_cols = history.shape[3]
    tile_rows = owned_rows * lax.axis_size("src")
    row_count = tile_rows // block_edge
    col_count = halves * owned_rows // block_edge
    slot_blocks = blocks[0, 0, 0]
    slot_places = coords[0, 0, 0]
    live_slots = lax.iota(jnp.int32, slot_count) < counts[0, 0, 0]
    masked = jnp.where(live_slots[:, None, None], slot_blocks, jnp.zeros_like(slot_blocks))
    dense_tile = jnp.zeros((row_count, col_count, block_edge, block_edge), slot_blocks.dtype)
    dense_tile = dense_tile.at[slot_places[:, 0], slot_places[:, 1]].set(masked)
    lagged = history[0]
    first_bin = lax.axis_index("delay") == 0
    step_count = excitation.shape[0]
    results = []
    for moment in range(step_count):
        pieces = lagged.reshape(col_count, block_edge, excite_cols)
        summed = jnp.einsum("rcij,cjw->riw", dense_tile, pieces, preferred_element_type=jnp.float32)
        partial_value = summed.reshape(tile_rows, excite_cols)
        over_bins = lax.psum(partial_value.astype(jnp.bfloat16), "delay").astype(jnp.float32)
        field_rows = lax.psum_scatter(over_bins, "src", scatter_dimension=0, tiled=True)
        drive_rows = (excitation[moment, 0].astype(jnp.float32) - field_rows).astype(jnp.bfloat16)
        drive_rows = drive_rows.reshape(owned_rows // block_edge, block_edge, excite_cols)
        current = jnp.einsum(
            "bij,bjw->biw", inverse[0], drive_rows, preferred_element_type=jnp.float32
        )
        current = current.reshape(owned_rows, excite_cols).astype(jnp.bfloat16)
        results.append(current)
        if moment + 1 < step_count:
            newest = lax.all_gather(current[None], "tgt", axis=0, tiled=True)
            shifted = from_behind(lagged, "delay", 1)
            lagged = jnp.where(first_bin, newest, shifted)
    return jnp.stack(results)[:, None]


def solution(mesh):
    placed = (
        P("delay", "src", "tgt", None, None, None),
        P("delay", "src", "tgt", None, None),
        P("delay", "src", "tgt"),
        P("delay", None, "src", None),
        P(None, "tgt", "src", None),
        P("tgt", "src", None, None),
    )
    return jax.shard_map(
        shards, mesh=mesh, in_specs=placed, out_specs=P(None, "tgt", "src", None), check_vma=False
    )
```

profile of v0, /device:TPU:1, one launch (start us, length us, event | category | flops | bytes accessed | tf_op | source)
XLA Modules:
  0.0 790.6 jit_solution(921665008089031722)
XLA Ops:
  7.2 0.8 fusion.21
  8.0 1.4 bitcast_select_fusion
  9.4 5.4 broadcast_in_dim.21
  14.7 5.0 scatter_fusion
  19.8 23.2 %copy.10 = bf16[32,128,8,128]{3,2,1,0:T(8,128)(2,1)} copy(bf16[32,128,8,128]{3,1,2,0:T(8,128)(2,1)} %bitcast.47) | data formatting | bytes 16777216 | tf_op jit(solution)/shard_map/rcij,cjw->riw/dot_general | solution.py:34
  43.0 6.9 fusion.13
  49.8 0.0 reduce-scatter.3.cloned.1.call-start
  49.9 294.8 %all-reduce.3.cloned.1.call-done = bf16[4096,128]{1,0:T(8,128)(2,1)} async-done(((bf16[4096,128]{1,0:T(8,128)(2,1)}), bf16[4096,128]{1,0:T(8,128)(2,1)}) %all-reduce.3.cloned.1.call-update) | async-done | bytes 1048592 | tf_op jit(solution)/shard_map/psum | solution.py:36
  344.7 2.7 convert_element_type.65
  347.4 0.0 reduce-scatter.3.cloned.1.call-update
  347.4 0.0 all-reduce.5.cloned.1.call-start
  347.5 3.1 collective-permute-start
  350.6 61.2 %reduce-scatter.3.cloned.1.call-done = f32[512,128]{1,0:T(8,128)} async-done(((f32[4096,128]{1,0:T(8,128)}), f32[512,128]{1,0:T(8,128)}) %reduce-scatter.3.cloned.1.call-update) | async-done | bytes 262160 | tf_op jit(solution)/shard_map/reduce_scatter | solution.py:37
  411.8 1.0 fusion.17
  412.7 0.2 convolution_convert_fusion.1
  412.9 7.4 all_gather.3
  420.4 6.8 fusion.10
  427.2 0.0 reduce-scatter.5.cloned.1.call-start
  427.2 288.1 %all-reduce.5.cloned.1.call-done = bf16[4096,128]{1,0:T(8,128)(2,1)} async-done(((bf16[4096,128]{1,0:T(8,128)(2,1)}), bf16[4096,128]{1,0:T(8,128)(2,1)}) %all-reduce.5.cloned.1.call-update) | async-done | bytes 1048592 | tf_op jit(solution)/shard_map/psum | solution.py:36
  715.3 2.7 convert_element_type.73
  718.1 64.2 %reduce-scatter.5.cloned.1.call-done = f32[512,128]{1,0:T(8,128)} async-done(((f32[4096,128]{1,0:T(8,128)}), f32[512,128]{1,0:T(8,128)}) %reduce-scatter.5.cloned.1.call-update) | async-done | bytes 262160 | tf_op jit(solution)/shard_map/reduce_scatter | solution.py:37
  782.2 1.0 fusion.16
  783.2 0.2 convolution_convert_fusion
  783.4 0.7 maximum_bitcast_fusion
  (13 shorter events, 0.1 us)
Async XLA Ops:
  6.5 406.2 %copy-start = (bf16[1,4,128,128]{3,2,1,0:T(8,128)(2,1)S(1)}, bf16[1,4,128,128]{3,2,1,0:T(8,128)(2,1)}, u32[]{:S(2)}) copy-start(bf16[1,4,128,128]{3,2,1,0:T(8,128)(2,1)} %param.11) | copy-start | bytes 393220
  6.5 338.1 %all-reduce.3.cloned.1.call-start = ((), (), s32[]{:S(2)}) async-start(), calls=%async_computation.2 | async-start | bytes 2097152 | tf_op jit(solution)/shard_map/psum | solution.py:36
  19.8 23.2 %copy-start.2 = (bf16[1,2,512,128]{3,2,1,0:T(8,128)(2,1)S(1)}, bf16[1,2,512,128]{3,2,1,0:T(8,128)(2,1)}, u32[]{:S(2)}) copy-start(bf16[1,2,512,128]{3,2,1,0:T(8,128)(2,1)} %param.9) | copy-start | bytes 786436
  43.0 368.8 %copy-start.1 = (bf16[2,1,512,128]{3,2,1,0:T(8,128)(2,1)S(1)}, bf16[2,1,512,128]{3,2,1,0:T(8,128)(2,1)}, u32[]{:S(2)}) copy-start(bf16[2,1,512,128]{3,2,1,0:T(8,128)(2,1)} %param.10) | copy-start | bytes 786436
  49.8 361.9 %reduce-scatter.3.cloned.1.call-start = ((), (), s32[]{:S(2)}) async-start(), calls=%async_computation.3 | async-start | bytes 2359296 | tf_op jit(solution)/shard_map/reduce_scatter | solution.py:37
  347.4 367.9 %all-reduce.5.cloned.1.call-start = ((), (), s32[]{:S(2)}) async-start(), calls=%async_computation.4 | async-start | bytes 2097152 | tf_op jit(solution)/shard_map/psum | solution.py:36
  347.5 72.9 %collective-permute-start = (bf16[2,512,128]{2,1,0:T(8,128)(2,1)S(1)}, bf16[2,512,128]{2,1,0:T(8,128)(2,1)S(1)}, u32[]{:S(2)}, u32[]{:S(2)}) collective-permute-start(bf16[2,512,128]{2,1,0:T(8,128)(2,1)S(1)} %bitcast.57), channel_id=1, source_target_pairs={{0,16},{16,32},{32,48},{48,64},{64,80},{80,96},{96,112},{112,128},... | collective-permute-start | bytes 786440 | tf_op jit(solution)/shard_map/ppermute | solution.py:10
  427.2 355.0 %reduce-scatter.5.cloned.1.call-start = ((), (), s32[]{:S(2)}) async-start(), calls=%async_computation.5 | async-start | bytes 2359296 | tf_op jit(solution)/shard_map/reduce_scatter | solution.py:37
Sparse Core Ops, SparseCore 0:
  50.0 294.6 all-reduce.2
  347.6 64.1 reduce-scatter.2
  427.3 288.0 all-reduce.4
  718.2 63.9 reduce-scatter.4
where the time goes:
time: 795 us; the launch traced here: 791 us
  waiting for transfers between devices  708 us (89%)
  local copies, waits for them, and re-layouts  33.6 us (4%)
  matrix products  14 us (2%)
  between operations  13.9 us (2%)
  other arithmetic  10.3 us (1%)
    psum x2, waiting for transfers between devices, shards(): lax.psum(partial_value.astype(jnp.bfloat16), 'delay').astype(jnp.float32)  583 us
    reduce_scatter x2, waiting for transfers between devices, shards(): lax.psum_scatter(over_bins, 'src', scatter_dimension=0, tiled=True)  125 us
    dot_general x1, local copies, waits for them, and re-layouts, shards(): jnp.einsum('rcij,cjw->riw', dense_tile, pieces, preferred_element_type=jn...  23.2 us
  transfers between devices with their start and end apart: 5, of which 4 were waited for; matrix products, arithmetic and copies ran while one was open for 0% of the time, Pallas kernels for 0%

commit v1 on v0

v1 whole, which is shorter than its diff:
```python
import functools

import jax
import jax.numpy as jnp
from jax import lax
from jax.experimental import pallas as pl
from jax.experimental.pallas import tpu as pltpu
from jax.sharding import PartitionSpec as P

MESH = pl.DeviceIdType.MESH
F32 = jnp.float32
BF16 = jnp.bfloat16


def rcopy(src, dst, send, recv, device):
    return pltpu.make_async_remote_copy(
        src_ref=src, dst_ref=dst, send_sem=send, recv_sem=recv, device_id=device, device_id_type=MESH
    )


def drain(ref, sem):
    pltpu.make_async_copy(ref, ref, sem).wait()


def loop(count, body):
    def step(i, carry):
        body(i)
        return carry

    lax.fori_loop(0, count, step, 0)


def kernel(
    K, Y,
    idx, key, blocks, hist, exc, inv, out,
    bv, xv, ev, iv, pa, pb, ra, rb, qa, qb, sa, sb, zs, zr, dv, sl, kv, ad, us, ur, ov,
    ld, a1s, a1r, b1s, b1r, a2s, a2r, b2s, b2r, zss, zrs, gss, grs, uss, urs, hs, hr, cs, cr, os,
):
    k, s, h = lax.axis_index("delay"), lax.axis_index("src"), lax.axis_index("tgt")
    Z = K // 2
    S = 2 * Y
    zi = 128 // Z
    z, xh = k // 2, k % 2
    xl, y = s // Y, s % Y
    x = xh * 2 + xl
    e = s * 2 + h

    def at_x(other):
        return (z * 2 + other // 2, (other % 2) * Y + y, h)

    def at_y(other):
        return (k, xl * Y + other, h)

    loads = [
        pltpu.make_async_copy(blocks, bv.at[pl.ds(0, 32)], ld.at[0]),
        pltpu.make_async_copy(hist, xv.at[0], ld.at[1]),
        pltpu.make_async_copy(inv, iv, ld.at[2]),
    ]
    for step in range(2):
        for bb in range(2):
            loads.append(pltpu.make_async_copy(
                exc.at[step, 2 * xh + bb, pl.ds(z * zi, zi)], ev.at[step, bb], ld.at[3 + step * 2 + bb]))
    for copy in loads:
        copy.start()
    bv[32] = jnp.zeros((128, 128), BF16)

    barrier = pltpu.get_barrier_semaphore()
    loop(K - 1, lambda i: pl.semaphore_signal(
        barrier, inc=1, device_id=((k + 1 + i) % K, s, h), device_id_type=MESH))

    def greet(i):
        other = (e + 1 + i) % (2 * S)
        pl.semaphore_signal(barrier, inc=1, device_id=(k, other // 2, other % 2), device_id_type=MESH)

    loop(2 * S - 1, greet)
    pl.semaphore_signal(barrier, inc=1, device_id=at_x(3 - x), device_id_type=MESH)
    for copy in loads:
        copy.wait()
    pl.semaphore_wait(barrier, (K - 1) + (2 * S - 1) + 1)

    @pl.when(k == 0)
    def _():
        def give(i):
            other = 1 + i
            rcopy(blocks.at[:, pl.ds(other * zi, zi)], sl.at[h], cs.at[0], cr.at[0], (other * 2, s, h)).start()
            rcopy(key, kv.at[h], cs.at[1], cr.at[1], (other * 2, s, h)).start()

        loop(Z - 1, give)
        mine = pltpu.make_async_copy(blocks.at[:, pl.ds(0, zi)], sl.at[h], cr.at[0])
        mine.start()
        also = pltpu.make_async_copy(key, kv.at[h], cr.at[1])
        also.start()

    def row_block(xx, yy, bb):
        return 4 * ((xx % 2) * Y + yy) + 2 * (xx // 2) + bb

    def block_sum(step, r):
        total = None
        for jp in range(4):
            left = bv[idx[r * 8 + 2 * jp]]
            right = bv[idx[r * 8 + 2 * jp + 1]]
            term = jnp.dot(jnp.concatenate([left, right], axis=1), xv[step, jp], preferred_element_type=F32)
            total = term if total is None else total + term
        return total.astype(BF16)

    def first_stage(step, live):
        for i in range(4):
            dx = (i + 2) % 4
            xx = (x + dx) % 4

            def fill_a(u):
                if live is None:
                    pa[step, xx, u] = block_sum(step, row_block(xx, u, 0))
                else:
                    @pl.when(live)
                    def _():
                        pa[step, xx, u] = block_sum(step, row_block(xx, u, 0))

                    @pl.when(jnp.logical_not(live))
                    def _():
                        pa[step, xx, u] = jnp.zeros((128, 128), BF16)

            loop(Y, fill_a)
            if dx:
                rcopy(pa.at[step, xx], ra.at[step, dx - 1], a1s.at[step, dx - 1], a1r.at[step, dx - 1], at_x(xx)).start()
            if i < Y:
                dy = (i + Y // 2) % Y
                yy = (y + dy) % Y

                def fill_b(u):
                    if live is None:
                        pb[step, yy, u] = block_sum(step, row_block(u, yy, 1))
                    else:
                        @pl.when(live)
                        def _():
                            pb[step, yy, u] = block_sum(step, row_block(u, yy, 1))

                        @pl.when(jnp.logical_not(live))
                        def _():
                            pb[step, yy, u] = jnp.zeros((128, 128), BF16)

                loop(4, fill_b)
                if dy:
                    rcopy(pb.at[step, yy], rb.at[step, dy - 1], b1s.at[step, dy - 1], b1r.at[step, dy - 1], at_y(yy)).start()

    def second_stage(step):
        for d in range(3):
            drain(ra.at[step, d], a1r.at[step, d])
        total = pa[step, x].astype(F32)
        for d in range(3):
            total += ra[step, d].astype(F32)
        qa[step] = total.astype(BF16)
        for dy in [Y // 2] + [d for d in range(1, Y) if d != Y // 2]:
            yy = (y + dy) % Y
            rcopy(qa.at[step, yy], sa.at[step, dy - 1], a2s.at[step, dy - 1], a2r.at[step, dy - 1], at_y(yy)).start()
        for d in range(Y - 1):
            drain(rb.at[step, d], b1r.at[step, d])
        total = pb[step, y].astype(F32)
        for d in range(Y - 1):
            total += rb[step, d].astype(F32)
        qb[step] = total.astype(BF16)
        for dx in (2, 1, 3):
            xx = (x + dx) % 4
            rcopy(qb.at[step, xx], sb.at[step, dx - 1], b2s.at[step, dx - 1], b2r.at[step, dx - 1], at_x(xx)).start()

    def far_first(i):
        return Z // 2 + (1 - 2 * (i % 2)) * ((i + 1) // 2)

    def third_stage(step):
        for d in range(Y - 1):
            drain(sa.at[step, d], a2r.at[step, d])
        first = qa[step, y].astype(F32)
        for d in range(Y - 1):
            first += sa[step, d].astype(F32)
        for d in range(3):
            drain(sb.at[step, d], b2r.at[step, d])
        second = qb[step, x].astype(F32)
        for d in range(3):
            second += sb[step, d].astype(F32)
        both = jnp.concatenate([first.reshape(Z, zi, 128), second.reshape(Z, zi, 128)], axis=1)
        zs[step] = both.astype(BF16)

        def give(i):
            other = (z + far_first(i)) % Z
            rcopy(zs.at[step, other], zr.at[step, z], zss.at[step], zrs.at[step], (other * 2 + xh, s, h)).start()

        loop(Z - 1, give)

    def field(step):
        drain(zr.at[step, pl.ds(0, Z - 1)], zrs.at[step])
        zr[step, z] = zs[step, z]
        return jnp.sum(zr[step].astype(F32), axis=0)

    def gather(step, total):
        incident = jnp.concatenate([ev[step, 0].astype(F32), ev[step, 1].astype(F32)], axis=0)
        dv[step, xh * Z + z] = (incident - total).astype(BF16)
        here = dv.at[step, xh * Z + z]

        def give(i):
            other = (z + far_first(i)) % Z
            rcopy(here, here, gss.at[step], grs.at[step], (other * 2 + (1 - xh), s, h)).start()
            rcopy(here, here, gss.at[step], grs.at[step], (other * 2 + xh, s, h)).start()

        loop(Z - 1, give)
        rcopy(here, here, gss.at[step], grs.at[step], (z * 2 + (1 - xh), s, h)).start()

    def currents(step):
        drain(dv.at[step, pl.ds(0, K - 1)], grs.at[step])
        for half in range(2):
            chunk = dv[step, half * Z:(half + 1) * Z].astype(F32)
            for bb in range(2):
                drive = chunk[:, bb * zi:(bb + 1) * zi, :].reshape(128, 128).astype(BF16)
                b = 2 * half + bb
                ov[step, b] = jnp.dot(iv[b], drive, preferred_element_type=F32).astype(BF16)
        pltpu.make_async_copy(ov.at[step], out.at[step], os.at[step]).start()

    first_stage(0, None)

    mine = pl.ds(2 * h, 2)

    @pl.when(k < K - 1)
    def _():
        rcopy(hist.at[mine], xv.at[1, mine], hs.at[0], hr.at[0], (k + 1, s, h)).start()

    second_stage(0)

    @pl.when(xh == 0)
    def _():
        drain(sl.at[h], cr.at[0])
        drain(kv.at[h], cr.at[1])
        rcopy(sl.at[h], sl.at[h], cs.at[2], cr.at[0], (k + 1, s, h)).start()
        rcopy(kv.at[h], kv.at[h], cs.at[3], cr.at[1], (k + 1, s, h)).start()
        rcopy(sl.at[h], sl.at[h], cs.at[4], cr.at[2], (k, s, 1 - h)).start()
        rcopy(kv.at[h], kv.at[h], cs.at[5], cr.at[3], (k, s, 1 - h)).start()

    @pl.when(k > 0)
    def _():
        drain(xv.at[1, mine], hr.at[0])
        rcopy(xv.at[1, mine], xv.at[1, mine], hs.at[1], hr.at[1], (k, s, 1 - h)).start()

    third_stage(0)

    @pl.when(k > 0)
    def _():
        drain(xv.at[1, pl.ds(2 - 2 * h, 2)], hr.at[1])

    first_stage(1, k > 0)
    gather(0, field(0))

    @pl.when(xh == 1)
    def _():
        drain(sl.at[h], cr.at[0])
        drain(kv.at[h], cr.at[1])
        rcopy(sl.at[h], sl.at[h], cs.at[4], cr.at[2], (k, s, 1 - h)).start()
        rcopy(kv.at[h], kv.at[h], cs.at[5], cr.at[3], (k, s, 1 - h)).start()

    second_stage(1)

    drain(sl.at[1 - h], cr.at[2])
    drain(kv.at[1 - h], cr.at[3])
    rows, wide = S * 2 * zi, 32 * zi
    m = lax.broadcasted_iota(jnp.int32, (rows, wide), 0)
    n = lax.broadcasted_iota(jnp.int32, (rows, wide), 1)
    q = m // zi
    place = (4 * (q // 2) + 2 * xh + q % 2) * 8 + 4 * h
    same = (m % zi) == (n % zi)
    for half in range(2):
        slots = sl[half].astype(F32).reshape(wide, 128).astype(BF16)
        where = jnp.broadcast_to(kv[half, 0:1, :], (rows, wide))
        for jj in range(4):
            pick = jnp.where(same & (where == place + jj), 1.0, 0.0).astype(BF16)
            ad[half, :, jj * 128:(jj + 1) * 128] = jnp.dot(pick, slots, preferred_element_type=F32).astype(BF16)

    third_stage(1)
    currents(0)

    newest = ov[0].reshape(512, 128)
    for half in range(2):
        made = jnp.dot(ad[half], newest, preferred_element_type=F32).astype(BF16)
        for other in range(S):
            us[other * 2 + half] = made[other * 2 * zi:(other + 1) * 2 * zi]

    def share(i):
        other = (e + 1 + i) % (2 * S)
        rcopy(us.at[other], ur.at[e], uss.at[0], urs.at[0], (k, other // 2, other % 2)).start()

    loop(2 * S - 1, share)
    rest = field(1)
    drain(ur.at[pl.ds(0, 2 * S - 1)], urs.at[0])
    ur[e] = us[e]
    gather(1, rest + jnp.sum(ur[...].astype(F32), axis=0))
    currents(1)

    for step in range(2):
        for d in range(3):
            drain(pa.at[step, 0], a1s.at[step, d])
            drain(qb.at[step, 0], b2s.at[step, d])
        for d in range(Y - 1):
            drain(pb.at[step, 0], b1s.at[step, d])
            drain(qa.at[step, 0], a2s.at[step, d])
        drain(zs.at[step, pl.ds(0, Z - 1)], zss.at[step])
        drain(dv.at[step, pl.ds(0, K - 1)], gss.at[step])
    drain(us.at[pl.ds(0, 2 * S - 1)], uss.at[0])

    @pl.when(k < K - 1)
    def _():
        drain(xv.at[1, mine], hs.at[0])

    @pl.when(k > 0)
    def _():
        drain(xv.at[1, mine], hs.at[1])

    @pl.when(k == 0)
    def _():
        drain(bv.at[pl.ds(0, 32 - 32 // Z)], cs.at[0])
        drain(dv.at[0, pl.ds(0, 2 * Z - 2)], cs.at[1])

    @pl.when(xh == 0)
    def _():
        drain(sl.at[h], cs.at[2])
        drain(kv.at[h], cs.at[3])

    drain(sl.at[h], cs.at[4])
    drain(kv.at[h], cs.at[5])
    for step in range(2):
        pltpu.make_async_copy(ov.at[step], out.at[step], os.at[step]).wait()


def shards(K, S, blocks, coords, counts, history, excitation, inverse):
    Y, Z = S // 2, K // 2
    zi = 128 // Z
    slots = lax.iota(jnp.int32, 32)
    places = coords[0, 0, 0]
    key = jnp.where(slots < counts[0, 0, 0], places[:, 0] * 8 + places[:, 1], -1)
    cells = lax.iota(jnp.int32, 4 * S * 8)
    idx = jnp.min(jnp.where(key[:, None] == cells[None, :], slots[:, None], 32), axis=0)
    wide = jnp.broadcast_to(key[None, :, None], (8, 32, zi)).reshape(8, 32 * zi)
    dma = pltpu.SemaphoreType.DMA
    v = pltpu.VMEM
    scratch = [
        v((33, 128, 128), BF16), v((2, 4, 256, 128), BF16), v((2, 2, zi, 128), BF16), v((4, 128, 128), BF16),
        v((2, 4, Y, 128, 128), BF16), v((2, Y, 4, 128, 128), BF16),
        v((2, 3, Y, 128, 128), BF16), v((2, Y - 1, 4, 128, 128), BF16),
        v((2, Y, 128, 128), BF16), v((2, 4, 128, 128), BF16),
        v((2, Y - 1, 128, 128), BF16), v((2, 3, 128, 128), BF16),
        v((2, Z, 2 * zi, 128), BF16), v((2, Z, 2 * zi, 128), BF16), v((2, K, 2 * zi, 128), BF16),
        v((2, 32, zi, 128), BF16), v((2, 8, 32 * zi), jnp.int32), v((2, S * 2 * zi, 512), BF16),
        v((2 * S, 2 * zi, 128), BF16), v((2 * S, 2 * zi, 128), BF16), v((2, 4, 128, 128), BF16),
        dma((7,)), dma((2, 3)), dma((2, 3)), dma((2, Y - 1)), dma((2, Y - 1)),
        dma((2, Y - 1)), dma((2, Y - 1)), dma((2, 3)), dma((2, 3)),
        dma((2,)), dma((2,)), dma((2,)), dma((2,)), dma((1,)), dma((1,)), dma((2,)), dma((2,)), dma((6,)), dma((4,)), dma((2,)),
    ]
    any_ = pl.BlockSpec(memory_space=pl.ANY)
    made = pl.pallas_call(
        functools.partial(kernel, K, Y),
        out_shape=jax.ShapeDtypeStruct((2, 4, 128, 128), BF16),
        in_specs=[pl.BlockSpec(memory_space=pltpu.SMEM)] + [any_] * 5,
        out_specs=any_,
        scratch_shapes=scratch,
        compiler_params=pltpu.CompilerParams(
            collective_id=0, has_side_effects=True, vmem_limit_bytes=40 * 1024 * 1024),
        name="march",
    )(
        idx, wide, blocks[0, 0, 0], history[0].reshape(4, 256, 128),
        excitation[:, 0].reshape(2, 4, 128, 128), inverse[0],
    )
    return made.reshape(2, 1, 512, 128)


def solution(mesh):
    placed = (
        P("delay", "src", "tgt", None, None, None),
        P("delay", "src", "tgt", None, None),
        P("delay", "src", "tgt"),
        P("delay", None, "src", None),
        P(None, "tgt", "src", None),
        P("tgt", "src", None, None),
    )
    return jax.shard_map(
        functools.partial(shards, mesh.shape["delay"], mesh.shape["src"]),
        mesh=mesh, in_specs=placed, out_specs=P(None, "tgt", "src", None), check_vma=False,
    )
```

time: 795 us -> 79.3 us (0.10)
  waiting for transfers between devices: 708 us -> 0 us
  Pallas kernels: 0 us -> 72.7 us
  local copies, waits for them, and re-layouts: 33.6 us -> 5.56 us
  matrix products: 14 us -> 0 us
  between operations: 13.9 us -> 0.69 us
  other arithmetic: 10.3 us -> 0.1 us
    psum x2 -> x0, waiting for transfers between devices: 583 us -> none  [shards(): lax.psum(partial_value.astype(jnp.bfloat16), 'delay').astype(jnp.float32)]
    reduce_scatter x2 -> x0, waiting for transfers between devices: 125 us -> none  [shards(): lax.psum_scatter(over_bins, 'src', scatter_dimension=0, tiled=True)]
    pallas_call x0 -> x1, Pallas kernels: none -> 72.7 us  [shards(): pl.pallas_call(functools.partial(kernel, K, Y), out_shape=jax.ShapeDtypeS...]
    dot_general x1 -> x0, local copies, waits for them, and re-layouts: 23.2 us -> none  [shards(): jnp.einsum('rcij,cjw->riw', dense_tile, pieces, preferred_element_type=jn...]
    dot_general x4 -> x0, matrix products: 14 us -> none  [the longest x2 13.6 us: shards(): jnp.einsum('rcij,cjw->riw', dense_tile, pieces, preferred_element_type=jn...]
  transfers between devices with their start and end apart: 5 -> 0, of which waited for: 4 -> 0; matrix products, arithmetic and copies ran while one was open for 0% -> 0% of each run, Pallas kernels for 0% -> 0%
where the time goes in v1:
time: 79.3 us; the launch traced here: 79.1 us
  Pallas kernels  72.7 us (92%)
  local copies, waits for them, and re-layouts  5.56 us (7%)
    pallas_call x1, Pallas kernels, shards(): pl.pallas_call(functools.partial(kernel, K, Y), out_shape=jax.ShapeDtypeS...  72.7 us
    unnamed x11, local copies, waits for them, and re-layouts  5.4 us

profile of v1, /device:TPU:1, one launch (start us, length us, event | category | flops | bytes accessed | tf_op | source)
XLA Modules:
  0.0 79.1 jit_solution(17158499937851948804)
XLA Ops:
  0.7 0.0 copy-start.4
  0.7 0.7 copy-done.4
  1.3 0.1 select_reduce_fusion.idx
  1.4 0.1 broadcast_in_dim.35
  1.5 0.1 broadcast_in_dim.36
  1.6 0.0 copy-start
  1.6 1.2 %copy-done = bf16[1,1,1,32,128,128]{5,4,3,2,1,0:T(8,128)(2,1)S(1)} copy-done((bf16[1,1,1,32,128,128]{5,4,3,2,1,0:T(8,128)(2,1)S(1)}, bf16[1,1,1,32,128,128]{5,4,3,2,1,0:T(8,128)(2,1)}, u32[]{:S(2)}) %copy-start) | copy-done | bytes 1048600
  2.8 0.0 copy-start.1
  2.8 0.9 %copy-done.1 = bf16[1,2,512,128]{3,2,1,0:T(8,128)(2,1)S(1)} copy-done((bf16[1,2,512,128]{3,2,1,0:T(8,128)(2,1)S(1)}, bf16[1,2,512,128]{3,2,1,0:T(8,128)(2,1)}, u32[]{:S(2)}) %copy-start.1) | copy-done | bytes 262168
  3.8 0.0 copy-start.2
  3.8 0.9 %copy-done.2 = bf16[2,1,512,128]{3,2,1,0:T(8,128)(2,1)S(1)} copy-done((bf16[2,1,512,128]{3,2,1,0:T(8,128)(2,1)S(1)}, bf16[2,1,512,128]{3,2,1,0:T(8,128)(2,1)}, u32[]{:S(2)}) %copy-start.2) | copy-done | bytes 262168
  4.7 0.0 copy-start.3
  4.7 0.9 %copy-done.3 = bf16[1,4,128,128]{3,2,1,0:T(8,128)(2,1)S(1)} copy-done((bf16[1,4,128,128]{3,2,1,0:T(8,128)(2,1)S(1)}, bf16[1,4,128,128]{3,2,1,0:T(8,128)(2,1)}, u32[]{:S(2)}) %copy-start.3) | copy-done | bytes 131096
  5.6 72.7 %march.1 = bf16[2,4,128,128]{3,2,1,0:T(8,128)(2,1)S(1)} custom-call(s32[256]{0:T(256)S(1)} %select_reduce_fusion.idx, s32[8,256]{1,0:T(8,128)S(1)} %broadcast_in_dim.37.key, bf16[32,128,128]{2,1,0:T(8,128)(2,1)S(1)} %bitcast.15, bf16[4,256,128]{2,1,0:T(8,128)(2,1)S(1)} %bitcast.17, bf16[2,4,128,128]{3,2,1,0:T(8,128)(2,1)S(1)} %bitcast.18, ...), custom_call_target="tpu_custom_call" | custom-call | tf_op jit(solution)/shard_map/march/pallas_call | solution.py:354
  78.4 0.7 copy.12
  (3 shorter events, 0.0 us)
Async XLA Ops:
  0.7 0.7 copy-start.4
  1.6 1.2 %copy-start = (bf16[1,1,1,32,128,128]{5,4,3,2,1,0:T(8,128)(2,1)S(1)}, bf16[1,1,1,32,128,128]{5,4,3,2,1,0:T(8,128)(2,1)}, u32[]{:S(2)}) copy-start(bf16[1,1,1,32,128,128]{5,4,3,2,1,0:T(8,128)(2,1)} %param.6) | copy-start | bytes 3145732
  2.8 0.9 %copy-start.1 = (bf16[1,2,512,128]{3,2,1,0:T(8,128)(2,1)S(1)}, bf16[1,2,512,128]{3,2,1,0:T(8,128)(2,1)}, u32[]{:S(2)}) copy-start(bf16[1,2,512,128]{3,2,1,0:T(8,128)(2,1)} %param.9) | copy-start | bytes 786436
  3.8 0.9 %copy-start.2 = (bf16[2,1,512,128]{3,2,1,0:T(8,128)(2,1)S(1)}, bf16[2,1,512,128]{3,2,1,0:T(8,128)(2,1)}, u32[]{:S(2)}) copy-start(bf16[2,1,512,128]{3,2,1,0:T(8,128)(2,1)} %param.10) | copy-start | bytes 786436
  4.7 0.9 %copy-start.3 = (bf16[1,4,128,128]{3,2,1,0:T(8,128)(2,1)S(1)}, bf16[1,4,128,128]{3,2,1,0:T(8,128)(2,1)}, u32[]{:S(2)}) copy-start(bf16[1,4,128,128]{3,2,1,0:T(8,128)(2,1)} %param.11) | copy-start | bytes 393220

commit v2 on v1

v2 whole, which is shorter than its diff:
```python
import functools

import jax
import jax.numpy as jnp
from jax import lax
from jax.experimental import pallas as pl
from jax.experimental.pallas import tpu as pltpu
from jax.sharding import PartitionSpec as P

MESH = pl.DeviceIdType.MESH
F32 = jnp.float32
BF16 = jnp.bfloat16


def rcopy(src, dst, send, recv, device):
    return pltpu.make_async_remote_copy(
        src_ref=src, dst_ref=dst, send_sem=send, recv_sem=recv, device_id=device, device_id_type=MESH
    )


def drain(ref, sem):
    pltpu.make_async_copy(ref, ref, sem).wait()


def wrap(value, size):
    return lax.rem(value, size)


def loop(count, body):
    def step(i, carry):
        body(i)
        return carry

    lax.fori_loop(0, count, step, 0)


def kernel(
    K, Y,
    tab, key, blocks, hist, exc, inv, out,
    bv, x0, x1, ev, iv, acc, dr, pa, pb, ra, rb, qa, qb, sa, sb, zs, zr, dv, sl, kv, ad, us, ur, ov,
    ld, a1s, a1r, b1s, b1r, a2s, a2r, b2s, b2r, zss, zrs, gss, grs, uss, urs, hs, hr, cs, cr, os,
):
    k, s, h = lax.axis_index("delay"), lax.axis_index("src"), lax.axis_index("tgt")
    Z = K // 2
    S = 2 * Y
    zi = 128 // Z
    z, xh = lax.div(k, 2), lax.rem(k, 2)
    xl, y = lax.div(s, Y), lax.rem(s, Y)
    x = xh * 2 + xl
    e = s * 2 + h

    def at_x(other):
        return (z * 2 + lax.div(other, 2), lax.rem(other, 2) * Y + y, h)

    def at_y(other):
        return (k, xl * Y + other, h)

    loads = [
        pltpu.make_async_copy(blocks, bv, ld.at[0]),
        pltpu.make_async_copy(hist, x0, ld.at[1]),
        pltpu.make_async_copy(inv, iv, ld.at[2]),
    ]
    for step in range(2):
        for bb in range(2):
            loads.append(pltpu.make_async_copy(
                exc.at[step, 2 * xh + bb, pl.ds(z * zi, zi)], ev.at[step, bb], ld.at[3 + step * 2 + bb]))
    for copy in loads:
        copy.start()

    barrier = pltpu.get_barrier_semaphore()

    def greet(device):
        pl.semaphore_signal(barrier, inc=1, device_id=device, device_id_type=MESH)

    for d in range(1, K):
        greet((wrap(k + d, K), s, h))
    for d in range(1, 2 * S):
        other = wrap(e + d, 2 * S)
        greet((k, lax.div(other, 2), lax.rem(other, 2)))
    greet(at_x(3 - x))

    acc[32] = jnp.zeros((128, 128), F32)

    def products(tile):
        def body(g):
            total = acc[wrap(4 * g + 32, 33)]
            for c in range(4):
                c = 4 * g + c
                made = jnp.dot(bv[tab[c]], tile[tab[32 + c]], preferred_element_type=F32)
                total = made + total * tab[64 + c].astype(F32)
                acc[c] = total

        loop(8, body)

    loads[0].wait()
    loads[1].wait()
    products(x0)
    for copy in loads[2:]:
        copy.wait()
    pl.semaphore_wait(barrier, (K - 1) + (2 * S - 1) + 1)

    @pl.when(k == 0)
    def _():
        def give(i):
            other = 1 + i
            rcopy(blocks.at[:, pl.ds(other * zi, zi)], sl.at[h], cs.at[0], cr.at[0], (other * 2, s, h)).start()
            rcopy(key, kv.at[h], cs.at[1], cr.at[1], (other * 2, s, h)).start()

        loop(Z - 1, give)
        mine = pltpu.make_async_copy(blocks.at[:, pl.ds(0, zi)], sl.at[h], cr.at[0])
        mine.start()
        also = pltpu.make_async_copy(key, kv.at[h], cr.at[1])
        also.start()

    def row_block(xx, yy, bb):
        return 4 * (lax.rem(xx, 2) * Y + yy) + 2 * lax.div(xx, 2) + bb

    def first_stage(step):
        for i in range(4):
            dx = (i + 2) % 4
            xx = wrap(x + dx, 4)

            def fill_a(u):
                pa[step, xx, u] = acc[tab[96 + row_block(xx, u, 0)]].astype(BF16)

            loop(Y, fill_a)
            if dx:
                rcopy(pa.at[step, xx], ra.at[step, dx - 1], a1s.at[step, dx - 1], a1r.at[step, dx - 1], at_x(xx)).start()
            if i < Y:
                dy = (i + Y // 2) % Y
                yy = wrap(y + dy, Y)

                def fill_b(u):
                    pb[step, yy, u] = acc[tab[96 + row_block(u, yy, 1)]].astype(BF16)

                loop(4, fill_b)
                if dy:
                    rcopy(pb.at[step, yy], rb.at[step, dy - 1], b1s.at[step, dy - 1], b1r.at[step, dy - 1], at_y(yy)).start()

    def second_stage(step):
        for d in range(3):
            drain(ra.at[step, d], a1r.at[step, d])
        total = pa[step, x].astype(F32)
        for d in range(3):
            total += ra[step, d].astype(F32)
        qa[step] = total.astype(BF16)
        for dy in [Y // 2] + [d for d in range(1, Y) if d != Y // 2]:
            yy = wrap(y + dy, Y)
            rcopy(qa.at[step, yy], sa.at[step, dy - 1], a2s.at[step, dy - 1], a2r.at[step, dy - 1], at_y(yy)).start()
        for d in range(Y - 1):
            drain(rb.at[step, d], b1r.at[step, d])
        total = pb[step, y].astype(F32)
        for d in range(Y - 1):
            total += rb[step, d].astype(F32)
        qb[step] = total.astype(BF16)
        for dx in (2, 1, 3):
            xx = wrap(x + dx, 4)
            rcopy(qb.at[step, xx], sb.at[step, dx - 1], b2s.at[step, dx - 1], b2r.at[step, dx - 1], at_x(xx)).start()

    def far_first(i):
        return Z // 2 + (1 - 2 * lax.rem(i, 2)) * lax.div(i + 1, 2)

    def third_stage(step):
        for d in range(Y - 1):
            drain(sa.at[step, d], a2r.at[step, d])
        first = qa[step, y].astype(F32)
        for d in range(Y - 1):
            first += sa[step, d].astype(F32)
        for d in range(3):
            drain(sb.at[step, d], b2r.at[step, d])
        second = qb[step, x].astype(F32)
        for d in range(3):
            second += sb[step, d].astype(F32)
        both = jnp.concatenate([first.reshape(Z, zi, 128), second.reshape(Z, zi, 128)], axis=1)
        zs[step] = both.astype(BF16)

        def give(i):
            other = wrap(z + far_first(i), Z)
            rcopy(zs.at[step, other], zr.at[step, z], zss.at[step], zrs.at[step], (other * 2 + xh, s, h)).start()

        loop(Z - 1, give)

    def field(step):
        drain(zr.at[step, pl.ds(0, Z - 1)], zrs.at[step])
        zr[step, z] = zs[step, z]
        return jnp.sum(zr[step].astype(F32), axis=0)

    def gather(step, total):
        incident = jnp.concatenate([ev[step, 0].astype(F32), ev[step, 1].astype(F32)], axis=0)
        dv[step, xh * Z + z] = (incident - total).astype(BF16)
        here = dv.at[step, xh * Z + z]

        if step == 0:
            def give(i):
                other = wrap(z + far_first(i), Z)
                for half in (1 - xh, xh):
                    rcopy(here, here, gss.at[step], grs.at[step], (other * 2 + half, s, h)).start()

            loop(Z - 1, give)
            rcopy(here, here, gss.at[step], grs.at[step], (z * 2 + (1 - xh), s, h)).start()
        else:
            rcopy(here, here, gss.at[step], grs.at[step], (z * 2 + (1 - xh), s, h)).start()

            def hand(i):
                other = i + (z <= i).astype(jnp.int32)
                for half in (1 - xh, xh):
                    rcopy(here, here, gss.at[step], grs.at[step], (other * 2 + half, s, h)).start()

            loop(Z - 1, hand)

    def driven(step):
        drain(dv.at[step, pl.ds(0, K - 1)], grs.at[step])
        for half in range(2):
            chunk = dv[step, half * Z:(half + 1) * Z].astype(F32)
            for bb in range(2):
                dr[step, 2 * half + bb] = chunk[:, bb * zi:(bb + 1) * zi, :].reshape(128, 128).astype(BF16)
        pltpu.make_async_copy(dr.at[step], out.at[step], os.at[step]).start()

    first_stage(0)

    mine = pl.ds(4 * h, 4)

    @pl.when(k < K - 1)
    def _():
        rcopy(hist.at[mine], x1.at[mine], hs.at[0], hr.at[0], (k + 1, s, h)).start()

    second_stage(0)

    @pl.when(xh == 0)
    def _():
        drain(sl.at[h], cr.at[0])
        drain(kv.at[h], cr.at[1])
        rcopy(sl.at[h], sl.at[h], cs.at[2], cr.at[0], (k + 1, s, h)).start()
        rcopy(kv.at[h], kv.at[h], cs.at[3], cr.at[1], (k + 1, s, h)).start()
        rcopy(sl.at[h], sl.at[h], cs.at[4], cr.at[2], (k, s, 1 - h)).start()
        rcopy(kv.at[h], kv.at[h], cs.at[5], cr.at[3], (k, s, 1 - h)).start()

    @pl.when(k > 0)
    def _():
        drain(x1.at[mine], hr.at[0])
        rcopy(x1.at[mine], x1.at[mine], hs.at[1], hr.at[1], (k, s, 1 - h)).start()

    third_stage(0)

    @pl.when(k > 0)
    def _():
        drain(x1.at[pl.ds(4 - 4 * h, 4)], hr.at[1])

    @pl.when(k > 0)
    def _():
        products(x1)

    @pl.when(k == 0)
    def _():
        def clear(c):
            acc[c] = jnp.zeros((128, 128), F32)

        loop(32, clear)

    first_stage(1)
    gather(0, field(0))

    @pl.when(xh == 1)
    def _():
        drain(sl.at[h], cr.at[0])
        drain(kv.at[h], cr.at[1])
        rcopy(sl.at[h], sl.at[h], cs.at[4], cr.at[2], (k, s, 1 - h)).start()
        rcopy(kv.at[h], kv.at[h], cs.at[5], cr.at[3], (k, s, 1 - h)).start()

    second_stage(1)

    drain(sl.at[1 - h], cr.at[2])
    drain(kv.at[1 - h], cr.at[3])
    rows, wide = S * 2 * zi, 32 * zi
    m = lax.broadcasted_iota(jnp.int32, (rows, wide), 0)
    n = lax.broadcasted_iota(jnp.int32, (rows, wide), 1)
    q = m // zi
    place = (4 * (q // 2) + 2 * xh + q % 2) * 8 + 4 * h
    same = (m % zi) == (n % zi)
    for half in range(2):
        slots = sl[half].astype(F32).reshape(wide, 128).astype(BF16)
        where = jnp.broadcast_to(kv[half, 0:1, :], (rows, wide))
        for jj in range(4):
            pick = jnp.where(same & (where == place + jj), 1.0, 0.0).astype(BF16)
            ad[half, :, jj * 128:(jj + 1) * 128] = jnp.dot(pick, slots, preferred_element_type=F32).astype(BF16)

    third_stage(1)
    driven(0)
    for b in range(4):
        ov[b * 128:(b + 1) * 128] = jnp.dot(iv[b], dr[0, b], preferred_element_type=F32).astype(BF16)
    newest = ov[...]
    for half in range(2):
        made = jnp.dot(ad[half], newest, preferred_element_type=F32).astype(BF16)
        for other in range(S):
            us[other * 2 + half] = made[other * 2 * zi:(other + 1) * 2 * zi]

    for d in list(range(S, 2 * S)) + list(range(1, S)):
        other = wrap(e + d, 2 * S)
        rcopy(us.at[other], ur.at[e], uss.at[0], urs.at[0], (k, lax.div(other, 2), lax.rem(other, 2))).start()

    rest = field(1)
    drain(ur.at[pl.ds(0, 2 * S - 1)], urs.at[0])
    ur[e] = us[e]
    gather(1, rest + jnp.sum(ur[...].astype(F32), axis=0))
    driven(1)

    for step in range(2):
        for d in range(3):
            drain(pa.at[step, 0], a1s.at[step, d])
            drain(qb.at[step, 0], b2s.at[step, d])
        for d in range(Y - 1):
            drain(pb.at[step, 0], b1s.at[step, d])
            drain(qa.at[step, 0], a2s.at[step, d])
        drain(zs.at[step, pl.ds(0, Z - 1)], zss.at[step])
        drain(dv.at[step, pl.ds(0, K - 1)], gss.at[step])
    drain(us.at[pl.ds(0, 2 * S - 1)], uss.at[0])

    @pl.when(k < K - 1)
    def _():
        drain(x1.at[mine], hs.at[0])

    @pl.when(k > 0)
    def _():
        drain(x1.at[mine], hs.at[1])

    @pl.when(k == 0)
    def _():
        drain(bv.at[pl.ds(0, 32 - 32 // Z)], cs.at[0])
        drain(dv.at[0, pl.ds(0, 2 * Z - 2)], cs.at[1])

    @pl.when(xh == 0)
    def _():
        drain(sl.at[h], cs.at[2])
        drain(kv.at[h], cs.at[3])

    drain(sl.at[h], cs.at[4])
    drain(kv.at[h], cs.at[5])
    for step in range(2):
        pltpu.make_async_copy(dr.at[step], out.at[step], os.at[step]).wait()


def shards(K, S, blocks, coords, counts, history, excitation, inverse):
    Y, Z = S // 2, K // 2
    zi = 128 // Z
    slots = lax.iota(jnp.int32, 32)
    places = coords[0, 0, 0]
    key = jnp.where(slots < counts[0, 0, 0], places[:, 0] * 8 + places[:, 1], 1 << 20)
    ahead = (key[None, :] < key[:, None]) | ((key[None, :] == key[:, None]) & (slots[None, :] < slots[:, None]))
    rank = jnp.sum(ahead.astype(jnp.int32), axis=1)
    chosen = rank[None, :] == slots[:, None]
    order = jnp.sum(jnp.where(chosen, slots[None, :], 0), axis=1)
    placed = jnp.sum(jnp.where(chosen, key[None, :], 0), axis=1)
    row = placed // 8
    before = jnp.sum(jnp.where(rank[None, :] == slots[:, None] - 1, key[None, :] // 8, 0), axis=1)
    keep = ((slots > 0) & (row == before)).astype(jnp.int32)
    last = jnp.max(jnp.where(key[None, :] // 8 == lax.iota(jnp.int32, 4 * S)[:, None], rank[None, :], -1), axis=1)
    last = jnp.where(last < 0, 32, last)
    tab = jnp.concatenate([order, placed % 8, keep, last])
    wide = jnp.broadcast_to(key[None, :, None], (8, 32, zi)).reshape(8, 32 * zi)
    dma = pltpu.SemaphoreType.DMA
    v = pltpu.VMEM
    scratch = [
        v((32, 128, 128), BF16), v((8, 128, 128), BF16), v((8, 128, 128), BF16), v((2, 2, zi, 128), BF16), v((4, 128, 128), BF16),
        v((33, 128, 128), F32), v((2, 4, 128, 128), BF16),
        v((2, 4, Y, 128, 128), BF16), v((2, Y, 4, 128, 128), BF16),
        v((2, 3, Y, 128, 128), BF16), v((2, Y - 1, 4, 128, 128), BF16),
        v((2, Y, 128, 128), BF16), v((2, 4, 128, 128), BF16),
        v((2, Y - 1, 128, 128), BF16), v((2, 3, 128, 128), BF16),
        v((2, Z, 2 * zi, 128), BF16), v((2, Z, 2 * zi, 128), BF16), v((2, K, 2 * zi, 128), BF16),
        v((2, 32, zi, 128), BF16), v((2, 8, 32 * zi), jnp.int32), v((2, S * 2 * zi, 512), BF16),
        v((2 * S, 2 * zi, 128), BF16), v((2 * S, 2 * zi, 128), BF16), v((512, 128), BF16),
        dma((7,)), dma((2, 3)), dma((2, 3)), dma((2, Y - 1)), dma((2, Y - 1)),
        dma((2, Y - 1)), dma((2, Y - 1)), dma((2, 3)), dma((2, 3)),
        dma((2,)), dma((2,)), dma((2,)), dma((2,)), dma((1,)), dma((1,)), dma((2,)), dma((2,)), dma((6,)), dma((4,)), dma((2,)),
    ]
    hbm = pl.BlockSpec(memory_space=pltpu.HBM)
    made = pl.pallas_call(
        functools.partial(kernel, K, Y),
        out_shape=jax.ShapeDtypeStruct((2, 4, 128, 128), BF16),
        in_specs=[pl.BlockSpec(memory_space=pltpu.SMEM)] + [hbm] * 5,
        out_specs=pl.BlockSpec(memory_space=pl.ANY),
        scratch_shapes=scratch,
        compiler_params=pltpu.CompilerParams(
            collective_id=0, has_side_effects=True, vmem_limit_bytes=67043328),
        name="march",
    )(
        tab, wide, blocks[0, 0, 0], history[0].reshape(8, 128, 128),
        excitation[:, 0].reshape(2, 4, 128, 128), inverse[0],
    )
    both = jnp.broadcast_to(inverse[0][None], made.shape)
    currents = jnp.einsum("nbij,nbjw->nbiw", both, made, preferred_element_type=F32)
    return currents.astype(BF16).reshape(2, 1, 512, 128)


def solution(mesh):
    placed = (
        P("delay", "src", "tgt", None, None, None),
        P("delay", "src", "tgt", None, None),
        P("delay", "src", "tgt"),
        P("delay", None, "src", None),
        P(None, "tgt", "src", None),
        P("tgt", "src", None, None),
    )
    return jax.shard_map(
        functools.partial(shards, mesh.shape["delay"], mesh.shape["src"]),
        mesh=mesh, in_specs=placed, out_specs=P(None, "tgt", "src", None), check_vma=False,
    )
```

time: 79.3 us -> 74.9 us (0.945)
  local copies, waits for them, and re-layouts: 5.56 us -> 1.44 us
  Pallas kernels: 72.7 us -> 69.4 us
  matrix products: 0 us -> 1.94 us
  other arithmetic: 0.1 us -> 1.1 us
    unnamed x11 -> x2, local copies, waits for them, and re-layouts: 5.4 us -> 0.67 us
    pallas_call x1, Pallas kernels: 72.7 us -> 69.4 us  [shards(): pl.pallas_call(functools.partial(kernel, K, Y), out_shape=jax.ShapeDtypeS...]
    dot_general x0 -> x1, matrix products: none -> 1.94 us  [shards(): jnp.einsum('nbij,nbjw->nbiw', both, made, preferred_element_type=F32)]
where the time goes in v2:
time: 74.9 us; the launch traced here: 74.6 us
  Pallas kernels  69.4 us (93%)
  matrix products  1.94 us (3%)
  local copies, waits for them, and re-layouts  1.44 us (2%)
  other arithmetic  1.1 us (1%)
    pallas_call x1, Pallas kernels, shards(): pl.pallas_call(functools.partial(kernel, K, Y), out_shape=jax.ShapeDtypeS...  69.4 us
    dot_general x1, matrix products, shards(): jnp.einsum('nbij,nbjw->nbiw', both, made, preferred_element_type=F32)  1.94 us

profile of v2, /device:TPU:1, one launch (start us, length us, event | category | flops | bytes accessed | tf_op | source)
XLA Modules:
  0.0 74.6 jit_solution(3501121502417229066)
XLA Ops:
  0.7 0.0 copy-start
  0.7 0.7 copy-done
  1.4 0.2 convert_reduce_fusion
  1.5 0.2 select_reduce_fusion.1
  1.8 0.7 pad_add_fusion.tab
  2.4 0.1 broadcast_in_dim.73
  2.5 0.1 broadcast_in_dim.74
  2.6 0.6 broadcast_in_dim.75.key
  3.2 69.4 %march.1 = bf16[2,4,128,128]{3,2,1,0:T(8,128)(2,1)} custom-call(s32[128]{0:T(128)} %pad_add_fusion.tab, s32[8,256]{1,0:T(8,128)} %broadcast_in_dim.75.key, bf16[32,128,128]{2,1,0:T(8,128)(2,1)} %bitcast.19, bf16[8,128,128]{2,1,0:T(8,128)(2,1)} %bitcast.22, bf16[2,4,128,128]{3,2,1,0:T(8,128)(2,1)} %bitcast.23, bf16[4,128,128]{2,1,0:T(8,128)(2,1)} %bitcast.20), custom_call_target="tpu_custom_call" | custom-call | tf_op jit(solution)/shard_map/march/pallas_call | solution.py:377
  72.6 1.9 %convolution_convert_fusion = bf16[2,4,128,128]{2,3,1,0:T(8,128)(2,1)} fusion(bf16[2,4,128,128]{3,2,1,0:T(8,128)(2,1)} %march.1, bf16[4,128,128]{2,1,0:T(8,128)(2,1)} %bitcast.21), kind=kOutput, calls=%fused_computation | convolution fusion | flops 33685504 | bytes 655360 | tf_op jit(solution)/shard_map/nbij,nbjw->nbiw/dot_general | solution.py:391
  (5 shorter events, 0.0 us)
Async XLA Ops:
  0.7 0.7 copy-start

commit v3 on v2

--- a/solution.py
+++ b/solution.py
@@ -37,7 +37,7 @@
 def kernel(
     K, Y,
     tab, key, blocks, hist, exc, inv, out,
-    bv, x0, x1, ev, iv, acc, dr, pa, pb, ra, rb, qa, qb, sa, sb, zs, zr, dv, sl, kv, ad, us, ur, ov,
+    bv, pk, x0, x1, ev, iv, acc, dr, pa, pb, ra, rb, qa, qb, sa, sb, zs, zr, dv, sl, kv, ad, us, ur, ov,
     ld, a1s, a1r, b1s, b1r, a2s, a2r, b2s, b2r, zss, zrs, gss, grs, uss, urs, hs, hr, cs, cr, os,
 ):
     k, s, h = lax.axis_index("delay"), lax.axis_index("src"), lax.axis_index("tgt")
@@ -98,19 +98,6 @@
     for copy in loads[2:]:
         copy.wait()
     pl.semaphore_wait(barrier, (K - 1) + (2 * S - 1) + 1)
-
-    @pl.when(k == 0)
-    def _():
-        def give(i):
-            other = 1 + i
-            rcopy(blocks.at[:, pl.ds(other * zi, zi)], sl.at[h], cs.at[0], cr.at[0], (other * 2, s, h)).start()
-            rcopy(key, kv.at[h], cs.at[1], cr.at[1], (other * 2, s, h)).start()
-
-        loop(Z - 1, give)
-        mine = pltpu.make_async_copy(blocks.at[:, pl.ds(0, zi)], sl.at[h], cr.at[0])
-        mine.start()
-        also = pltpu.make_async_copy(key, kv.at[h], cr.at[1])
-        also.start()
 
     def row_block(xx, yy, bb):
         return 4 * (lax.rem(xx, 2) * Y + yy) + 2 * lax.div(xx, 2) + bb
@@ -224,7 +211,41 @@
     def _():
         rcopy(hist.at[mine], x1.at[mine], hs.at[0], hr.at[0], (k + 1, s, h)).start()
 
+    @pl.when(k == 0)
+    def _():
+        def pack(c):
+            pk[:, c] = bv[c].astype(F32).reshape(Z, zi, 128).astype(BF16)
+
+        loop(32, pack)
+
+        def give(i):
+            other = 1 + i
+            rcopy(pk.at[other], sl.at[h], cs.at[0], cr.at[0], (other * 2, s, h)).start()
+            rcopy(key, kv.at[h], cs.at[1], cr.at[1], (other * 2, s, h)).start()
+
+        loop(Z - 1, give)
+        pltpu.make_async_copy(pk.at[0], sl.at[h], cr.at[0]).start()
+        pltpu.make_async_copy(key, kv.at[h], cr.at[1]).start()
+
     second_stage(0)
+    third_stage(0)
+
+    @pl.when(k > 0)
+    def _():
+        drain(x1.at[mine], hr.at[0])
+        rcopy(x1.at[mine], x1.at[mine], hs.at[1], hr.at[1], (k, s, 1 - h)).start()
+        drain(x1.at[pl.ds(4 - 4 * h, 4)], hr.at[1])
+        products(x1)
+
+    @pl.when(k == 0)
+    def _():
+        def clear(c):
+            acc[c] = jnp.zeros((128, 128), F32)
+
+        loop(32, clear)
+
+    first_stage(1)
+    gather(0, field(0))
 
     @pl.when(xh == 0)
     def _():
@@ -232,42 +253,17 @@
         drain(kv.at[h], cr.at[1])
         rcopy(sl.at[h], sl.at[h], cs.at[2], cr.at[0], (k + 1, s, h)).start()
         rcopy(kv.at[h], kv.at[h], cs.at[3], cr.at[1], (k + 1, s, h)).start()
-        rcopy(sl.at[h], sl.at[h], cs.at[4], cr.at[2], (k, s, 1 - h)).start()
-        rcopy(kv.at[h], kv.at[h], cs.at[5], cr.at[3], (k, s, 1 - h)).start()
-
-    @pl.when(k > 0)
-    def _():
-        drain(x1.at[mine], hr.at[0])
-        rcopy(x1.at[mine], x1.at[mine], hs.at[1], hr.at[1], (k, s, 1 - h)).start()
-
-    third_stage(0)
-
-    @pl.when(k > 0)
-    def _():
-        drain(x1.at[pl.ds(4 - 4 * h, 4)], hr.at[1])
-
-    @pl.when(k > 0)
-    def _():
-        products(x1)
-
-    @pl.when(k == 0)
-    def _():
-        def clear(c):
-            acc[c] = jnp.zeros((128, 128), F32)
-
-        loop(32, clear)
-
-    first_stage(1)
-    gather(0, field(0))
+
+    second_stage(1)
 
     @pl.when(xh == 1)
     def _():
         drain(sl.at[h], cr.at[0])
         drain(kv.at[h], cr.at[1])
-        rcopy(sl.at[h], sl.at[h], cs.at[4], cr.at[2], (k, s, 1 - h)).start()
-        rcopy(kv.at[h], kv.at[h], cs.at[5], cr.at[3], (k, s, 1 - h)).start()
-
-    second_stage(1)
+
+    rcopy(sl.at[h], sl.at[h], cs.at[4], cr.at[2], (k, s, 1 - h)).start()
+    rcopy(kv.at[h], kv.at[h], cs.at[5], cr.at[3], (k, s, 1 - h)).start()
+    third_stage(1)
 
     drain(sl.at[1 - h], cr.at[2])
     drain(kv.at[1 - h], cr.at[3])
@@ -284,7 +280,6 @@
             pick = jnp.where(same & (where == place + jj), 1.0, 0.0).astype(BF16)
             ad[half, :, jj * 128:(jj + 1) * 128] = jnp.dot(pick, slots, preferred_element_type=F32).astype(BF16)
 
-    third_stage(1)
     driven(0)
     for b in range(4):
         ov[b * 128:(b + 1) * 128] = jnp.dot(iv[b], dr[0, b], preferred_element_type=F32).astype(BF16)
@@ -337,6 +332,10 @@
     drain(kv.at[h], cs.at[5])
     for step in range(2):
         pltpu.make_async_copy(dr.at[step], out.at[step], os.at[step]).wait()
+
+
+def pin(array):
+    return pltpu.with_memory_space_constraint(array, pltpu.HBM)
 
 
 def shards(K, S, blocks, coords, counts, history, excitation, inverse):
@@ -360,7 +359,7 @@
     dma = pltpu.SemaphoreType.DMA
     v = pltpu.VMEM
     scratch = [
-        v((32, 128, 128), BF16), v((8, 128, 128), BF16), v((8, 128, 128), BF16), v((2, 2, zi, 128), BF16), v((4, 128, 128), BF16),
+        v((32, 128, 128), BF16), v((Z, 32, zi, 128), BF16), v((8, 128, 128), BF16), v((8, 128, 128), BF16), v((2, 2, zi, 128), BF16), v((4, 128, 128), BF16),
         v((33, 128, 128), F32), v((2, 4, 128, 128), BF16),
         v((2, 4, Y, 128, 128), BF16), v((2, Y, 4, 128, 128), BF16),
         v((2, 3, Y, 128, 128), BF16), v((2, Y - 1, 4, 128, 128), BF16),
@@ -377,15 +376,15 @@
     made = pl.pallas_call(
         functools.partial(kernel, K, Y),
         out_shape=jax.ShapeDtypeStruct((2, 4, 128, 128), BF16),
-        in_specs=[pl.BlockSpec(memory_space=pltpu.SMEM)] + [hbm] * 5,
+        in_specs=[pl.BlockSpec(memory_space=pltpu.SMEM), pl.BlockSpec(memory_space=pl.ANY)] + [hbm] * 4,
         out_specs=pl.BlockSpec(memory_space=pl.ANY),
         scratch_shapes=scratch,
         compiler_params=pltpu.CompilerParams(
-            collective_id=0, has_side_effects=True, vmem_limit_bytes=67043328),
+            collective_id=0, has_side_effects=True, vmem_limit_bytes=40 * 1024 * 1024),
         name="march",
     )(
-        tab, wide, blocks[0, 0, 0], history[0].reshape(8, 128, 128),
-        excitation[:, 0].reshape(2, 4, 128, 128), inverse[0],
+        tab, wide, pin(blocks[0, 0, 0]), pin(history[0].reshape(8, 128, 128)),
+        pin(excitation[:, 0].reshape(2, 4, 128, 128)), pin(inverse[0]),
     )
     both = jnp.broadcast_to(inverse[0][None], made.shape)
     currents = jnp.einsum("nbij,nbjw->nbiw", both, made, preferred_element_type=F32)

time: 74.9 us -> 66.9 us (0.89)
  Pallas kernels: 69.4 us -> 63.2 us
  matrix products: 1.94 us -> 0.92 us
    pallas_call x1, Pallas kernels: 69.4 us -> 63.2 us  [shards(): pl.pallas_call(functools.partial(kernel, K, Y), out_shape=jax.ShapeDtypeS...]
    dot_general x1, matrix products: 1.94 us -> 0.92 us  [shards(): jnp.einsum('nbij,nbjw->nbiw', both, made, preferred_element_type=F32)]
where the time goes in v3:
time: 66.9 us; the launch traced here: 66.2 us
  Pallas kernels  63.2 us (94%)
  matrix products  0.92 us (1%)
  local copies, waits for them, and re-layouts  0.84 us (1%)
  between operations  0.71 us (1%)
    pallas_call x1, Pallas kernels, shards(): pl.pallas_call(functools.partial(kernel, K, Y), out_shape=jax.ShapeDtypeS...  63.2 us

profile of v3, /device:TPU:1, one launch (start us, length us, event | category | flops | bytes accessed | tf_op | source)
XLA Modules:
  0.0 66.2 jit_solution(10363364638507920037)
XLA Ops:
  0.7 0.0 copy-start.1
  0.7 0.7 %copy-done.1 = s32[1,1,1,32,2]{3,4,2,1,0:T(2,128)S(1)} copy-done((s32[1,1,1,32,2]{3,4,2,1,0:T(2,128)S(1)}, s32[1,1,1,32,2]{3,4,2,1,0:T(2,128)}, u32[]{:S(2)}) %copy-start.1) | copy-done | bytes 280
  1.4 0.2 convert_reduce_fusion
  1.5 0.2 select_reduce_fusion.1
  1.8 0.1 pad_add_fusion.tab
  1.9 0.1 broadcast_in_dim.73
  1.9 0.1 broadcast_in_dim.74
  2.0 0.0 copy-start
  2.1 63.2 %march.1 = bf16[2,4,128,128]{3,2,1,0:T(8,128)(2,1)S(1)} custom-call(s32[128]{0:T(128)S(1)} %pad_add_fusion.tab, s32[8,256]{1,0:T(8,128)S(1)} %broadcast_in_dim.75.key, bf16[32,128,128]{2,1,0:T(8,128)(2,1)} %bitcast.19, bf16[8,128,128]{2,1,0:T(8,128)(2,1)} %bitcast.22, bf16[2,4,128,128]{3,2,1,0:T(8,128)(2,1)} %bitcast.23, bf16[4,128,128]{2,1,0:T(8,128)(2,1)} %bitcast.20), custom_call_target="tpu_custom_call" | custom-call | tf_op jit(solution)/shard_map/march/pallas_call | solution.py:376
  65.2 0.0 copy-done
  65.3 0.9 %convolution_convert_fusion = bf16[2,4,128,128]{2,3,1,0:T(8,128)(2,1)} fusion(bf16[2,4,128,128]{3,2,1,0:T(8,128)(2,1)S(1)} %march.1, bf16[4,128,128]{2,1,0:T(8,128)(2,1)S(1)} %bitcast.21), kind=kOutput, calls=%fused_computation | convolution fusion | flops 33685504 | bytes 655360 | tf_op jit(solution)/shard_map/nbij,nbjw->nbiw/dot_general | solution.py:390
  (6 shorter events, 0.0 us)
Async XLA Ops:
  0.7 0.7 %copy-start.1 = (s32[1,1,1,32,2]{3,4,2,1,0:T(2,128)S(1)}, s32[1,1,1,32,2]{3,4,2,1,0:T(2,128)}, u32[]{:S(2)}) copy-start(s32[1,1,1,32,2]{3,4,2,1,0:T(2,128)} %param.7) | copy-start | bytes 772
  2.0 63.2 %copy-start = (bf16[1,4,128,128]{3,2,1,0:T(8,128)(2,1)S(1)}, bf16[1,4,128,128]{3,2,1,0:T(8,128)(2,1)}, u32[]{:S(2)}) copy-start(bf16[1,4,128,128]{3,2,1,0:T(8,128)(2,1)} %param.11) | copy-start | bytes 393220

commit v4 on v3

--- a/solution.py
+++ b/solution.py
@@ -38,7 +38,7 @@
     K, Y,
     tab, key, blocks, hist, exc, inv, out,
     bv, pk, x0, x1, ev, iv, acc, dr, pa, pb, ra, rb, qa, qb, sa, sb, zs, zr, dv, sl, kv, ad, us, ur, ov,
-    ld, a1s, a1r, b1s, b1r, a2s, a2r, b2s, b2r, zss, zrs, gss, grs, uss, urs, hs, hr, cs, cr, os,
+    ld, a1s, a1r, b1s, b1r, a2s, a2r, b2s, b2r, zss, zrs, gss, grs, uss, urs, hs, hr, cs, cr, os, known,
 ):
     k, s, h = lax.axis_index("delay"), lax.axis_index("src"), lax.axis_index("tgt")
     Z = K // 2
@@ -72,12 +72,14 @@
     def greet(device):
         pl.semaphore_signal(barrier, inc=1, device_id=device, device_id_type=MESH)
 
-    for d in range(1, K):
-        greet((wrap(k + d, K), s, h))
     for d in range(1, 2 * S):
         other = wrap(e + d, 2 * S)
         greet((k, lax.div(other, 2), lax.rem(other, 2)))
+    greet((k + 1 - 2 * xh, s, h))
     greet(at_x(3 - x))
+    greet((wrap(k + 2 * xh - 1 + K, K), s, h))
+    greet((wrap(k + 2, K), s, h))
+    greet((wrap(k + K - 2, K), s, h))
 
     acc[32] = jnp.zeros((128, 128), F32)
 
@@ -92,12 +94,30 @@
 
         loop(8, body)
 
+    pl.semaphore_wait(barrier, (2 * S - 1) + 5)
+
+    def tell(turn):
+        for d in (1 << turn, Z - (1 << turn)):
+            pl.semaphore_signal(known.at[turn], inc=1, device_id=(wrap(z + d, Z) * 2 + xh, s, h), device_id_type=MESH)
+
+    def heard(turn):
+        pl.semaphore_wait(known.at[turn], 2)
+
+    turns = max(Z // 2, 1).bit_length() - 1
+    if turns > 0:
+        tell(0)
+
+    mine = pl.ds(4 * h, 4)
+
+    @pl.when(k < K - 1)
+    def _():
+        rcopy(hist.at[mine], x1.at[mine], hs.at[0], hr.at[0], (k + 1, s, h)).start()
+
     loads[0].wait()
     loads[1].wait()
     products(x0)
     for copy in loads[2:]:
         copy.wait()
-    pl.semaphore_wait(barrier, (K - 1) + (2 * S - 1) + 1)
 
     def row_block(xx, yy, bb):
         return 4 * (lax.rem(xx, 2) * Y + yy) + 2 * lax.div(xx, 2) + bb
@@ -205,11 +225,37 @@
 
     first_stage(0)
 
-    mine = pl.ds(4 * h, 4)
-
-    @pl.when(k < K - 1)
-    def _():
-        rcopy(hist.at[mine], x1.at[mine], hs.at[0], hr.at[0], (k + 1, s, h)).start()
+    if turns > 0:
+        heard(0)
+    if turns > 1:
+        tell(1)
+
+    @pl.when(k > 0)
+    def _():
+        drain(x1.at[mine], hr.at[0])
+        rcopy(x1.at[mine], x1.at[mine], hs.at[1], hr.at[1], (k, s, 1 - h)).start()
+
+    if turns > 1:
+        heard(1)
+    if turns > 2:
+        tell(2)
+    second_stage(0)
+    if turns > 2:
+        heard(2)
+
+    @pl.when(k > 0)
+    def _():
+        drain(x1.at[pl.ds(4 - 4 * h, 4)], hr.at[1])
+        products(x1)
+
+    @pl.when(k == 0)
+    def _():
+        def clear(c):
+            acc[c] = jnp.zeros((128, 128), F32)
+
+        loop(32, clear)
+
+    third_stage(0)
 
     @pl.when(k == 0)
     def _():
@@ -226,23 +272,6 @@
         loop(Z - 1, give)
         pltpu.make_async_copy(pk.at[0], sl.at[h], cr.at[0]).start()
         pltpu.make_async_copy(key, kv.at[h], cr.at[1]).start()
-
-    second_stage(0)
-    third_stage(0)
-
-    @pl.when(k > 0)
-    def _():
-        drain(x1.at[mine], hr.at[0])
-        rcopy(x1.at[mine], x1.at[mine], hs.at[1], hr.at[1], (k, s, 1 - h)).start()
-        drain(x1.at[pl.ds(4 - 4 * h, 4)], hr.at[1])
-        products(x1)
-
-    @pl.when(k == 0)
-    def _():
-        def clear(c):
-            acc[c] = jnp.zeros((128, 128), F32)
-
-        loop(32, clear)
 
     first_stage(1)
     gather(0, field(0))
@@ -371,6 +400,7 @@
         dma((7,)), dma((2, 3)), dma((2, 3)), dma((2, Y - 1)), dma((2, Y - 1)),
         dma((2, Y - 1)), dma((2, Y - 1)), dma((2, 3)), dma((2, 3)),
         dma((2,)), dma((2,)), dma((2,)), dma((2,)), dma((1,)), dma((1,)), dma((2,)), dma((2,)), dma((6,)), dma((4,)), dma((2,)),
+        pltpu.SemaphoreType.REGULAR((4,)),
     ]
     hbm = pl.BlockSpec(memory_space=pltpu.HBM)
     made = pl.pallas_call(

time: 66.9 us -> 79.9 us (1.19)
  Pallas kernels: 63.2 us -> 76.8 us
    pallas_call x1, Pallas kernels: 63.2 us -> 76.8 us  [shards(): pl.pallas_call(functools.partial(kernel, K, Y), out_shape=jax.ShapeDtypeS...]
where the time goes in v4:
time: 79.9 us; the launch traced here: 79.8 us
  Pallas kernels  76.8 us (96%)
  matrix products  0.92 us (1%)
  local copies, waits for them, and re-layouts  0.84 us (1%)
    pallas_call x1, Pallas kernels, shards(): pl.pallas_call(functools.partial(kernel, K, Y), out_shape=jax.ShapeDtypeS...  76.8 us

profile of v4, /device:TPU:1, one launch (start us, length us, event | category | flops | bytes accessed | tf_op | source)
XLA Modules:
  0.0 79.8 jit_solution(8593046197144906712)
XLA Ops:
  0.7 0.0 copy-start.1
  0.7 0.7 copy-done.1
  1.4 0.2 convert_reduce_fusion
  1.5 0.2 select_reduce_fusion.1
  1.8 0.1 pad_add_fusion.tab
  1.9 0.1 broadcast_in_dim.73
  1.9 0.1 broadcast_in_dim.74
  2.0 0.0 copy-start
  2.1 76.8 %march.1 = bf16[2,4,128,128]{3,2,1,0:T(8,128)(2,1)S(1)} custom-call(s32[128]{0:T(128)S(1)} %pad_add_fusion.tab, s32[8,256]{1,0:T(8,128)S(1)} %broadcast_in_dim.75.key, bf16[32,128,128]{2,1,0:T(8,128)(2,1)} %bitcast.19, bf16[8,128,128]{2,1,0:T(8,128)(2,1)} %bitcast.22, bf16[2,4,128,128]{3,2,1,0:T(8,128)(2,1)} %bitcast.23, bf16[4,128,128]{2,1,0:T(8,128)(2,1)} %bitcast.20), custom_call_target="tpu_custom_call" | custom-call | tf_op jit(solution)/shard_map/march/pallas_call | solution.py:406
  78.8 0.0 copy-done
  78.8 0.9 %convolution_convert_fusion = bf16[2,4,128,128]{2,3,1,0:T(8,128)(2,1)} fusion(bf16[2,4,128,128]{3,2,1,0:T(8,128)(2,1)S(1)} %march.1, bf16[4,128,128]{2,1,0:T(8,128)(2,1)S(1)} %bitcast.21), kind=kOutput, calls=%fused_computation | convolution fusion | flops 33685504 | bytes 655360 | tf_op jit(solution)/shard_map/nbij,nbjw->nbiw/dot_general | solution.py:420
  (6 shorter events, 0.0 us)
Async XLA Ops:
  0.7 0.7 copy-start.1
  2.0 76.8 %copy-start = (bf16[1,4,128,128]{3,2,1,0:T(8,128)(2,1)S(1)}, bf16[1,4,128,128]{3,2,1,0:T(8,128)(2,1)}, u32[]{:S(2)}) copy-start(bf16[1,4,128,128]{3,2,1,0:T(8,128)(2,1)} %param.11) | copy-start | bytes 393220

commit v5 on v4

--- a/solution.py
+++ b/solution.py
@@ -225,23 +225,38 @@
 
     first_stage(0)
 
-    if turns > 0:
-        heard(0)
-    if turns > 1:
-        tell(1)
+    @pl.when(k == 0)
+    def _():
+        def pack(c):
+            pk[:, c] = bv[c].astype(F32).reshape(Z, zi, 128).astype(BF16)
+
+        loop(32, pack)
+
+    def scatter(near, far):
+        @pl.when(k == 0)
+        def _():
+            if near == 0:
+                pltpu.make_async_copy(pk.at[0], sl.at[h], cr.at[0]).start()
+                pltpu.make_async_copy(key, kv.at[h], cr.at[1]).start()
+            for d in range(near + 1, far + 1):
+                for other in sorted({d, Z - d}):
+                    there = (other * 2 + 0, s, h)
+                    rcopy(pk.at[other], sl.at[h], cs.at[0], cr.at[0], there).start()
+                    rcopy(key, kv.at[h], cs.at[1], cr.at[1], there).start()
+
+    scatter(0, 1)
+    for turn in range(turns):
+        heard(turn)
+        if turn + 1 < turns:
+            tell(turn + 1)
+        scatter(1 << turn, 2 << turn)
 
     @pl.when(k > 0)
     def _():
         drain(x1.at[mine], hr.at[0])
         rcopy(x1.at[mine], x1.at[mine], hs.at[1], hr.at[1], (k, s, 1 - h)).start()
 
-    if turns > 1:
-        heard(1)
-    if turns > 2:
-        tell(2)
     second_stage(0)
-    if turns > 2:
-        heard(2)
 
     @pl.when(k > 0)
     def _():
@@ -256,23 +271,6 @@
         loop(32, clear)
 
     third_stage(0)
-
-    @pl.when(k == 0)
-    def _():
-        def pack(c):
-            pk[:, c] = bv[c].astype(F32).reshape(Z, zi, 128).astype(BF16)
-
-        loop(32, pack)
-
-        def give(i):
-            other = 1 + i
-            rcopy(pk.at[other], sl.at[h], cs.at[0], cr.at[0], (other * 2, s, h)).start()
-            rcopy(key, kv.at[h], cs.at[1], cr.at[1], (other * 2, s, h)).start()
-
-        loop(Z - 1, give)
-        pltpu.make_async_copy(pk.at[0], sl.at[h], cr.at[0]).start()
-        pltpu.make_async_copy(key, kv.at[h], cr.at[1]).start()
-
     first_stage(1)
     gather(0, field(0))
 
@@ -280,12 +278,12 @@
     def _():
         drain(sl.at[h], cr.at[0])
         drain(kv.at[h], cr.at[1])
-        rcopy(sl.at[h], sl.at[h], cs.at[2], cr.at[0], (k + 1, s, h)).start()
-        rcopy(kv.at[h], kv.at[h], cs.at[3], cr.at[1], (k + 1, s, h)).start()
+        rcopy(sl.at[h], sl.at[h], cs.at[2], cr.at[0], (k + 1 - 2 * xh, s, h)).start()
+        rcopy(kv.at[h], kv.at[h], cs.at[3], cr.at[1], (k + 1 - 2 * xh, s, h)).start()
 
     second_stage(1)
 
-    @pl.when(xh == 1)
+    @pl.when(xh != 0)
     def _():
         drain(sl.at[h], cr.at[0])
         drain(kv.at[h], cr.at[1])

time: 79.9 us -> 65.3 us (0.82)
  Pallas kernels: 76.8 us -> 61.6 us
    pallas_call x1, Pallas kernels: 76.8 us -> 61.6 us  [shards(): pl.pallas_call(functools.partial(kernel, K, Y), out_shape=jax.ShapeDtypeS...]
where the time goes in v5:
time: 65.3 us; the launch traced here: 64.6 us
  Pallas kernels  61.6 us (94%)
  matrix products  0.92 us (1%)
  local copies, waits for them, and re-layouts  0.84 us (1%)
  between operations  0.71 us (1%)
    pallas_call x1, Pallas kernels, shards(): pl.pallas_call(functools.partial(kernel, K, Y), out_shape=jax.ShapeDtypeS...  61.6 us

profile of v5, /device:TPU:1, one launch (start us, length us, event | category | flops | bytes accessed | tf_op | source)
XLA Modules:
  0.0 64.6 jit_solution(9459766312738226982)
XLA Ops:
  0.7 0.0 copy-start.1
  0.7 0.7 %copy-done.1 = s32[1,1,1,32,2]{3,4,2,1,0:T(2,128)S(1)} copy-done((s32[1,1,1,32,2]{3,4,2,1,0:T(2,128)S(1)}, s32[1,1,1,32,2]{3,4,2,1,0:T(2,128)}, u32[]{:S(2)}) %copy-start.1) | copy-done | bytes 280
  1.4 0.2 convert_reduce_fusion
  1.5 0.2 select_reduce_fusion.1
  1.8 0.1 pad_add_fusion.tab
  1.9 0.1 broadcast_in_dim.73
  1.9 0.1 broadcast_in_dim.74
  2.0 0.0 copy-start
  2.1 61.6 %march.1 = bf16[2,4,128,128]{3,2,1,0:T(8,128)(2,1)S(1)} custom-call(s32[128]{0:T(128)S(1)} %pad_add_fusion.tab, s32[8,256]{1,0:T(8,128)S(1)} %broadcast_in_dim.75.key, bf16[32,128,128]{2,1,0:T(8,128)(2,1)} %bitcast.19, bf16[8,128,128]{2,1,0:T(8,128)(2,1)} %bitcast.22, bf16[2,4,128,128]{3,2,1,0:T(8,128)(2,1)} %bitcast.23, bf16[4,128,128]{2,1,0:T(8,128)(2,1)} %bitcast.20), custom_call_target="tpu_custom_call" | custom-call | tf_op jit(solution)/shard_map/march/pallas_call | solution.py:404
  63.6 0.0 copy-done
  63.7 0.9 %convolution_convert_fusion = bf16[2,4,128,128]{2,3,1,0:T(8,128)(2,1)} fusion(bf16[2,4,128,128]{3,2,1,0:T(8,128)(2,1)S(1)} %march.1, bf16[4,128,128]{2,1,0:T(8,128)(2,1)S(1)} %bitcast.21), kind=kOutput, calls=%fused_computation | convolution fusion | flops 33685504 | bytes 655360 | tf_op jit(solution)/shard_map/nbij,nbjw->nbiw/dot_general | solution.py:418
  (6 shorter events, 0.0 us)
Async XLA Ops:
  0.7 0.7 %copy-start.1 = (s32[1,1,1,32,2]{3,4,2,1,0:T(2,128)S(1)}, s32[1,1,1,32,2]{3,4,2,1,0:T(2,128)}, u32[]{:S(2)}) copy-start(s32[1,1,1,32,2]{3,4,2,1,0:T(2,128)} %param.7) | copy-start | bytes 772
  2.0 61.6 %copy-start = (bf16[1,4,128,128]{3,2,1,0:T(8,128)(2,1)S(1)}, bf16[1,4,128,128]{3,2,1,0:T(8,128)(2,1)}, u32[]{:S(2)}) copy-start(bf16[1,4,128,128]{3,2,1,0:T(8,128)(2,1)} %param.11) | copy-start | bytes 393220

commit v6 on v5

--- a/solution.py
+++ b/solution.py
@@ -94,6 +94,10 @@
 
         loop(8, body)
 
+
+    loads[0].wait()
+    loads[1].wait()
+    products(x0)
     pl.semaphore_wait(barrier, (2 * S - 1) + 5)
 
     def tell(turn):
@@ -113,9 +117,6 @@
     def _():
         rcopy(hist.at[mine], x1.at[mine], hs.at[0], hr.at[0], (k + 1, s, h)).start()
 
-    loads[0].wait()
-    loads[1].wait()
-    products(x0)
     for copy in loads[2:]:
         copy.wait()
 
@@ -130,7 +131,8 @@
             def fill_a(u):
                 pa[step, xx, u] = acc[tab[96 + row_block(xx, u, 0)]].astype(BF16)
 
-            loop(Y, fill_a)
+            for u in range(Y):
+                fill_a(u)
             if dx:
                 rcopy(pa.at[step, xx], ra.at[step, dx - 1], a1s.at[step, dx - 1], a1r.at[step, dx - 1], at_x(xx)).start()
             if i < Y:
@@ -140,29 +142,32 @@
                 def fill_b(u):
                     pb[step, yy, u] = acc[tab[96 + row_block(u, yy, 1)]].astype(BF16)
 
-                loop(4, fill_b)
+                for u in range(4):
+                    fill_b(u)
                 if dy:
                     rcopy(pb.at[step, yy], rb.at[step, dy - 1], b1s.at[step, dy - 1], b1r.at[step, dy - 1], at_y(yy)).start()
 
     def second_stage(step):
         for d in range(3):
             drain(ra.at[step, d], a1r.at[step, d])
-        total = pa[step, x].astype(F32)
-        for d in range(3):
-            total += ra[step, d].astype(F32)
-        qa[step] = total.astype(BF16)
-        for dy in [Y // 2] + [d for d in range(1, Y) if d != Y // 2]:
+        for dy in [Y // 2] + [d for d in range(1, Y) if d != Y // 2] + [0]:
             yy = wrap(y + dy, Y)
-            rcopy(qa.at[step, yy], sa.at[step, dy - 1], a2s.at[step, dy - 1], a2r.at[step, dy - 1], at_y(yy)).start()
+            total = pa[step, x, yy].astype(F32)
+            for d in range(3):
+                total += ra[step, d, yy].astype(F32)
+            qa[step, yy] = total.astype(BF16)
+            if dy:
+                rcopy(qa.at[step, yy], sa.at[step, dy - 1], a2s.at[step, dy - 1], a2r.at[step, dy - 1], at_y(yy)).start()
         for d in range(Y - 1):
             drain(rb.at[step, d], b1r.at[step, d])
-        total = pb[step, y].astype(F32)
-        for d in range(Y - 1):
-            total += rb[step, d].astype(F32)
-        qb[step] = total.astype(BF16)
-        for dx in (2, 1, 3):
+        for dx in (2, 1, 3, 0):
             xx = wrap(x + dx, 4)
-            rcopy(qb.at[step, xx], sb.at[step, dx - 1], b2s.at[step, dx - 1], b2r.at[step, dx - 1], at_x(xx)).start()
+            total = pb[step, y, xx].astype(F32)
+            for d in range(Y - 1):
+                total += rb[step, d, xx].astype(F32)
+            qb[step, xx] = total.astype(BF16)
+            if dx:
+                rcopy(qb.at[step, xx], sb.at[step, dx - 1], b2s.at[step, dx - 1], b2r.at[step, dx - 1], at_x(xx)).start()
 
     def far_first(i):
         return Z // 2 + (1 - 2 * lax.rem(i, 2)) * lax.div(i + 1, 2)
@@ -324,8 +329,6 @@
     drain(ur.at[pl.ds(0, 2 * S - 1)], urs.at[0])
     ur[e] = us[e]
     gather(1, rest + jnp.sum(ur[...].astype(F32), axis=0))
-    driven(1)
-
     for step in range(2):
         for d in range(3):
             drain(pa.at[step, 0], a1s.at[step, d])
@@ -334,7 +337,6 @@
             drain(pb.at[step, 0], b1s.at[step, d])
             drain(qa.at[step, 0], a2s.at[step, d])
         drain(zs.at[step, pl.ds(0, Z - 1)], zss.at[step])
-        drain(dv.at[step, pl.ds(0, K - 1)], gss.at[step])
     drain(us.at[pl.ds(0, 2 * S - 1)], uss.at[0])
 
     @pl.when(k < K - 1)
@@ -357,6 +359,10 @@
 
     drain(sl.at[h], cs.at[4])
     drain(kv.at[h], cs.at[5])
+    drain(dv.at[0, pl.ds(0, K - 1)], gss.at[0])
+    driven(1)
+    drain(dv.at[1, pl.ds(0, K - 1)], gss.at[1])
+
     for step in range(2):
         pltpu.make_async_copy(dr.at[step], out.at[step], os.at[step]).wait()
 

time: 65.3 us -> 63.6 us (0.974)
  Pallas kernels: 61.6 us -> 60.4 us
    pallas_call x1, Pallas kernels: 61.6 us -> 60.4 us  [shards(): pl.pallas_call(functools.partial(kernel, K, Y), out_shape=jax.ShapeDtypeS...]
where the time goes in v6:
time: 63.6 us; the launch traced here: 63.4 us
  Pallas kernels  60.4 us (95%)
  matrix products  0.92 us (1%)
  local copies, waits for them, and re-layouts  0.84 us (1%)
  between operations  0.71 us (1%)
    pallas_call x1, Pallas kernels, shards(): pl.pallas_call(functools.partial(kernel, K, Y), out_shape=jax.ShapeDtypeS...  60.4 us

profile of v6, /device:TPU:1, one launch (start us, length us, event | category | flops | bytes accessed | tf_op | source)
XLA Modules:
  0.0 63.4 jit_solution(9104779100271696714)
XLA Ops:
  0.7 0.0 copy-start.1
  0.7 0.7 %copy-done.1 = s32[1,1,1,32,2]{3,4,2,1,0:T(2,128)S(1)} copy-done((s32[1,1,1,32,2]{3,4,2,1,0:T(2,128)S(1)}, s32[1,1,1,32,2]{3,4,2,1,0:T(2,128)}, u32[]{:S(2)}) %copy-start.1) | copy-done | bytes 280
  1.4 0.2 convert_reduce_fusion
  1.5 0.2 select_reduce_fusion.1
  1.8 0.1 pad_add_fusion.tab
  1.9 0.1 broadcast_in_dim.73
  1.9 0.1 broadcast_in_dim.74
  2.0 0.0 copy-start
  2.1 60.4 %march.1 = bf16[2,4,128,128]{3,2,1,0:T(8,128)(2,1)S(1)} custom-call(s32[128]{0:T(128)S(1)} %pad_add_fusion.tab, s32[8,256]{1,0:T(8,128)S(1)} %broadcast_in_dim.75.key, bf16[32,128,128]{2,1,0:T(8,128)(2,1)} %bitcast.19, bf16[8,128,128]{2,1,0:T(8,128)(2,1)} %bitcast.22, bf16[2,4,128,128]{3,2,1,0:T(8,128)(2,1)} %bitcast.23, bf16[4,128,128]{2,1,0:T(8,128)(2,1)} %bitcast.20), custom_call_target="tpu_custom_call" | custom-call | tf_op jit(solution)/shard_map/march/pallas_call | solution.py:410
  62.5 0.0 copy-done
  62.5 0.9 %convolution_convert_fusion = bf16[2,4,128,128]{2,3,1,0:T(8,128)(2,1)} fusion(bf16[2,4,128,128]{3,2,1,0:T(8,128)(2,1)S(1)} %march.1, bf16[4,128,128]{2,1,0:T(8,128)(2,1)S(1)} %bitcast.21), kind=kOutput, calls=%fused_computation | convolution fusion | flops 33685504 | bytes 655360 | tf_op jit(solution)/shard_map/nbij,nbjw->nbiw/dot_general | solution.py:424
  (6 shorter events, 0.0 us)
Async XLA Ops:
  0.7 0.7 %copy-start.1 = (s32[1,1,1,32,2]{3,4,2,1,0:T(2,128)S(1)}, s32[1,1,1,32,2]{3,4,2,1,0:T(2,128)}, u32[]{:S(2)}) copy-start(s32[1,1,1,32,2]{3,4,2,1,0:T(2,128)} %param.7) | copy-start | bytes 772
  2.0 60.4 %copy-start = (bf16[1,4,128,128]{3,2,1,0:T(8,128)(2,1)S(1)}, bf16[1,4,128,128]{3,2,1,0:T(8,128)(2,1)}, u32[]{:S(2)}) copy-start(bf16[1,4,128,128]{3,2,1,0:T(8,128)(2,1)} %param.11) | copy-start | bytes 393220

commit v7 on v6

--- a/solution.py
+++ b/solution.py
@@ -22,6 +22,10 @@
     pltpu.make_async_copy(ref, ref, sem).wait()
 
 
+def inside(value, size):
+    return jnp.minimum(jnp.maximum(value, 0), size - 1)
+
+
 def wrap(value, size):
     return lax.rem(value, size)
 
@@ -36,8 +40,8 @@
 
 def kernel(
     K, Y,
-    tab, key, blocks, hist, exc, inv, out,
-    bv, pk, x0, x1, ev, iv, acc, dr, pa, pb, ra, rb, qa, qb, sa, sb, zs, zr, dv, sl, kv, ad, us, ur, ov,
+    places, used, blocks, hist, exc, inv, out,
+    cv, tv, tab, key, bv, pk, x0, x1, ev, iv, acc, dr, pa, pb, ra, rb, qa, qb, sa, sb, zs, zr, dv, sl, kv, ad, us, ur, ov,
     ld, a1s, a1r, b1s, b1r, a2s, a2r, b2s, b2r, zss, zrs, gss, grs, uss, urs, hs, hr, cs, cr, os, known,
 ):
     k, s, h = lax.axis_index("delay"), lax.axis_index("src"), lax.axis_index("tgt")
@@ -55,6 +59,9 @@
     def at_y(other):
         return (k, xl * Y + other, h)
 
+    small = [
+        pltpu.make_async_copy(places, cv, ld.at[7]),
+    ]
     loads = [
         pltpu.make_async_copy(blocks, bv, ld.at[0]),
         pltpu.make_async_copy(hist, x0, ld.at[1]),
@@ -64,7 +71,7 @@
         for bb in range(2):
             loads.append(pltpu.make_async_copy(
                 exc.at[step, 2 * xh + bb, pl.ds(z * zi, zi)], ev.at[step, bb], ld.at[3 + step * 2 + bb]))
-    for copy in loads:
+    for copy in small + loads:
         copy.start()
 
     barrier = pltpu.get_barrier_semaphore()
@@ -81,15 +88,46 @@
     greet((wrap(k + 2, K), s, h))
     greet((wrap(k + K - 2, K), s, h))
 
+    for copy in small:
+        copy.wait()
+    shape = (32, 32)
+    sub = lax.broadcasted_iota(jnp.int32, shape, 0)
+    lane = lax.broadcasted_iota(jnp.int32, shape, 1)
+    spot = cv[0:1, :] * 8 + cv[1:2, :]
+    along = jnp.where(lane < used[0], jnp.broadcast_to(spot, shape), 1024)
+    down = jnp.broadcast_to(jnp.sum(jnp.where(sub == lane, along, 0), axis=1, keepdims=True), shape)
+    ahead = (along < down) | ((along == down) & (lane < sub))
+    rank = jnp.broadcast_to(jnp.sum(jnp.where(ahead, 1, 0), axis=1, keepdims=True), shape)
+    row = lax.div(down, 8)
+    chosen = rank == lane
+
+    def column_sum(mask, value):
+        return jnp.sum(jnp.where(mask, value, 0), axis=0, keepdims=True)
+
+    order = column_sum(chosen, sub)
+    column = column_sum(chosen, down - row * 8)
+    here = column_sum(chosen, row)
+    before = column_sum(rank == lane - 1, row + 1) - 1
+    keep = jnp.where(here == before, 1, 0)
+    last = jnp.max(jnp.where(row == lane, rank, -1), axis=0, keepdims=True)
+    last = jnp.where(last < 0, 32, last)
+    tv[...] = jnp.zeros((8, 128), jnp.int32)
+    for i, value in enumerate((order, column, keep, last)):
+        tv[i:i + 1, 0:32] = value
+    key[...] = jnp.full((8, 128), -1.0, F32)
+    key[0:1, 0:32] = along[0:1, :].astype(F32)
+    listed = pltpu.make_async_copy(tv, tab, ld.at[9])
+    listed.start()
     acc[32] = jnp.zeros((128, 128), F32)
+    listed.wait()
 
     def products(tile):
         def body(g):
             total = acc[wrap(4 * g + 32, 33)]
             for c in range(4):
                 c = 4 * g + c
-                made = jnp.dot(bv[tab[c]], tile[tab[32 + c]], preferred_element_type=F32)
-                total = made + total * tab[64 + c].astype(F32)
+                made = jnp.dot(bv[inside(tab[0, c], 32)], tile[inside(tab[1, c], 8)], preferred_element_type=F32)
+                total = made + total * tab[2, c].astype(F32)
                 acc[c] = total
 
         loop(8, body)
@@ -129,7 +167,7 @@
             xx = wrap(x + dx, 4)
 
             def fill_a(u):
-                pa[step, xx, u] = acc[tab[96 + row_block(xx, u, 0)]].astype(BF16)
+                pa[step, xx, u] = acc[inside(tab[3, row_block(xx, u, 0)], 33)].astype(BF16)
 
             for u in range(Y):
                 fill_a(u)
@@ -140,7 +178,7 @@
                 yy = wrap(y + dy, Y)
 
                 def fill_b(u):
-                    pb[step, yy, u] = acc[tab[96 + row_block(u, yy, 1)]].astype(BF16)
+                    pb[step, yy, u] = acc[inside(tab[3, row_block(u, yy, 1)], 33)].astype(BF16)
 
                 for u in range(4):
                     fill_b(u)
@@ -305,11 +343,15 @@
     q = m // zi
     place = (4 * (q // 2) + 2 * xh + q % 2) * 8 + 4 * h
     same = (m % zi) == (n % zi)
+    spread = jnp.where(
+        lax.broadcasted_iota(jnp.int32, (128, wide), 0) == lax.broadcasted_iota(jnp.int32, (128, wide), 1) // zi, 1.0, 0.0).astype(BF16)
+    place = place.astype(F32)
     for half in range(2):
         slots = sl[half].astype(F32).reshape(wide, 128).astype(BF16)
-        where = jnp.broadcast_to(kv[half, 0:1, :], (rows, wide))
+        named = jnp.dot(kv[half].astype(BF16), spread, preferred_element_type=F32)
+        where = jnp.broadcast_to(named[0:1, :], (rows, wide))
         for jj in range(4):
-            pick = jnp.where(same & (where == place + jj), 1.0, 0.0).astype(BF16)
+            pick = jnp.where(same & (where == place + float(jj)), 1.0, 0.0).astype(BF16)
             ad[half, :, jj * 128:(jj + 1) * 128] = jnp.dot(pick, slots, preferred_element_type=F32).astype(BF16)
 
     driven(0)
@@ -350,7 +392,7 @@
     @pl.when(k == 0)
     def _():
         drain(bv.at[pl.ds(0, 32 - 32 // Z)], cs.at[0])
-        drain(dv.at[0, pl.ds(0, 2 * Z - 2)], cs.at[1])
+        drain(acc.at[0, pl.ds(0, 8 * (Z - 1))], cs.at[1])
 
     @pl.when(xh == 0)
     def _():
@@ -374,24 +416,10 @@
 def shards(K, S, blocks, coords, counts, history, excitation, inverse):
     Y, Z = S // 2, K // 2
     zi = 128 // Z
-    slots = lax.iota(jnp.int32, 32)
-    places = coords[0, 0, 0]
-    key = jnp.where(slots < counts[0, 0, 0], places[:, 0] * 8 + places[:, 1], 1 << 20)
-    ahead = (key[None, :] < key[:, None]) | ((key[None, :] == key[:, None]) & (slots[None, :] < slots[:, None]))
-    rank = jnp.sum(ahead.astype(jnp.int32), axis=1)
-    chosen = rank[None, :] == slots[:, None]
-    order = jnp.sum(jnp.where(chosen, slots[None, :], 0), axis=1)
-    placed = jnp.sum(jnp.where(chosen, key[None, :], 0), axis=1)
-    row = placed // 8
-    before = jnp.sum(jnp.where(rank[None, :] == slots[:, None] - 1, key[None, :] // 8, 0), axis=1)
-    keep = ((slots > 0) & (row == before)).astype(jnp.int32)
-    last = jnp.max(jnp.where(key[None, :] // 8 == lax.iota(jnp.int32, 4 * S)[:, None], rank[None, :], -1), axis=1)
-    last = jnp.where(last < 0, 32, last)
-    tab = jnp.concatenate([order, placed % 8, keep, last])
-    wide = jnp.broadcast_to(key[None, :, None], (8, 32, zi)).reshape(8, 32 * zi)
     dma = pltpu.SemaphoreType.DMA
     v = pltpu.VMEM
     scratch = [
+        v((2, 32), jnp.int32), v((8, 128), jnp.int32), pltpu.SMEM((8, 128), jnp.int32), v((8, 128), F32),
         v((32, 128, 128), BF16), v((Z, 32, zi, 128), BF16), v((8, 128, 128), BF16), v((8, 128, 128), BF16), v((2, 2, zi, 128), BF16), v((4, 128, 128), BF16),
         v((33, 128, 128), F32), v((2, 4, 128, 128), BF16),
         v((2, 4, Y, 128, 128), BF16), v((2, Y, 4, 128, 128), BF16),
@@ -399,9 +427,9 @@
         v((2, Y, 128, 128), BF16), v((2, 4, 128, 128), BF16),
         v((2, Y - 1, 128, 128), BF16), v((2, 3, 128, 128), BF16),
         v((2, Z, 2 * zi, 128), BF16), v((2, Z, 2 * zi, 128), BF16), v((2, K, 2 * zi, 128), BF16),
-        v((2, 32, zi, 128), BF16), v((2, 8, 32 * zi), jnp.int32), v((2, S * 2 * zi, 512), BF16),
+        v((2, 32, zi, 128), BF16), v((2, 8, 128), F32), v((2, S * 2 * zi, 512), BF16),
         v((2 * S, 2 * zi, 128), BF16), v((2 * S, 2 * zi, 128), BF16), v((512, 128), BF16),
-        dma((7,)), dma((2, 3)), dma((2, 3)), dma((2, Y - 1)), dma((2, Y - 1)),
+        dma((10,)), dma((2, 3)), dma((2, 3)), dma((2, Y - 1)), dma((2, Y - 1)),
         dma((2, Y - 1)), dma((2, Y - 1)), dma((2, 3)), dma((2, 3)),
         dma((2,)), dma((2,)), dma((2,)), dma((2,)), dma((1,)), dma((1,)), dma((2,)), dma((2,)), dma((6,)), dma((4,)), dma((2,)),
         pltpu.SemaphoreType.REGULAR((4,)),
@@ -410,14 +438,14 @@
     made = pl.pallas_call(
         functools.partial(kernel, K, Y),
         out_shape=jax.ShapeDtypeStruct((2, 4, 128, 128), BF16),
-        in_specs=[pl.BlockSpec(memory_space=pltpu.SMEM), pl.BlockSpec(memory_space=pl.ANY)] + [hbm] * 4,
+        in_specs=[hbm, pl.BlockSpec(memory_space=pltpu.SMEM)] + [hbm] * 4,
         out_specs=pl.BlockSpec(memory_space=pl.ANY),
         scratch_shapes=scratch,
         compiler_params=pltpu.CompilerParams(
             collective_id=0, has_side_effects=True, vmem_limit_bytes=40 * 1024 * 1024),
         name="march",
     )(
-        tab, wide, pin(blocks[0, 0, 0]), pin(history[0].reshape(8, 128, 128)),
+        pin(coords[0, 0, 0].T), counts[0, 0], pin(blocks[0, 0, 0]), pin(history[0].reshape(8, 128, 128)),
         pin(excitation[:, 0].reshape(2, 4, 128, 128)), pin(inverse[0]),
     )
     both = jnp.broadcast_to(inverse[0][None], made.shape)

time: 63.6 us -> 61.8 us (0.972)
  local copies, waits for them, and re-layouts: 0.84 us -> 0.01 us
  Pallas kernels: 60.4 us -> 59.6 us
    pallas_call x1, Pallas kernels: 60.4 us -> 59.6 us  [shards(): pl.pallas_call(functools.partial(kernel, K, Y), out_shape=jax.ShapeDtypeS...]
    unnamed x4 -> x2, local copies, waits for them, and re-layouts: 0.68 us -> 0.01 us
where the time goes in v7:
time: 61.8 us; the launch traced here: 61.2 us
  Pallas kernels  59.6 us (96%)
  matrix products  0.92 us (1%)
  between operations  0.68 us (1%)
    pallas_call x1, Pallas kernels, shards(): pl.pallas_call(functools.partial(kernel, K, Y), out_shape=jax.ShapeDtypeS...  59.6 us

profile of v7, /device:TPU:1, one launch (start us, length us, event | category | flops | bytes accessed | tf_op | source)
XLA Modules:
  0.0 61.2 jit_solution(1909862363124639531)
XLA Ops:
  0.7 0.0 copy-start
  0.7 59.6 %march.1 = bf16[2,4,128,128]{3,2,1,0:T(8,128)(2,1)S(1)} custom-call(s32[2,32]{1,0:T(2,128)} %bitcast.20, s32[1]{0:T(128)} %bitcast.14.used, bf16[32,128,128]{2,1,0:T(8,128)(2,1)} %bitcast.15, bf16[8,128,128]{2,1,0:T(8,128)(2,1)} %bitcast.18, bf16[2,4,128,128]{3,2,1,0:T(8,128)(2,1)} %bitcast.19, bf16[4,128,128]{2,1,0:T(8,128)(2,1)} %bitcast.16), custom_call_target="tpu_custom_call" | custom-call | tf_op jit(solution)/shard_map/march/pallas_call | solution.py:438
  60.3 0.0 copy-done
  60.3 0.9 %convolution_convert_fusion = bf16[2,4,128,128]{2,3,1,0:T(8,128)(2,1)} fusion(bf16[2,4,128,128]{3,2,1,0:T(8,128)(2,1)S(1)} %march.1, bf16[4,128,128]{2,1,0:T(8,128)(2,1)S(1)} %bitcast.17), kind=kOutput, calls=%fused_computation | convolution fusion | flops 33685504 | bytes 655360 | tf_op jit(solution)/shard_map/nbij,nbjw->nbiw/dot_general | solution.py:452
Async XLA Ops:
  0.7 59.6 %copy-start = (bf16[1,4,128,128]{3,2,1,0:T(8,128)(2,1)S(1)}, bf16[1,4,128,128]{3,2,1,0:T(8,128)(2,1)}, u32[]{:S(2)}) copy-start(bf16[1,4,128,128]{3,2,1,0:T(8,128)(2,1)} %param.11) | copy-start | bytes 393220

commit v8 on v7

--- a/solution.py
+++ b/solution.py
@@ -132,7 +132,6 @@
 
         loop(8, body)
 
-
     loads[0].wait()
     loads[1].wait()
     products(x0)
@@ -151,10 +150,6 @@
 
     mine = pl.ds(4 * h, 4)
 
-    @pl.when(k < K - 1)
-    def _():
-        rcopy(hist.at[mine], x1.at[mine], hs.at[0], hr.at[0], (k + 1, s, h)).start()
-
     for copy in loads[2:]:
         copy.wait()
 
@@ -163,7 +158,7 @@
 
     def first_stage(step):
         for i in range(4):
-            dx = (i + 2) % 4
+            dx = (3, 2, 1, 0)[i]
             xx = wrap(x + dx, 4)
 
             def fill_a(u):
@@ -174,7 +169,7 @@
             if dx:
                 rcopy(pa.at[step, xx], ra.at[step, dx - 1], a1s.at[step, dx - 1], a1r.at[step, dx - 1], at_x(xx)).start()
             if i < Y:
-                dy = (i + Y // 2) % Y
+                dy = (Y - 1 - i) % Y
                 yy = wrap(y + dy, Y)
 
                 def fill_b(u):
@@ -267,6 +262,11 @@
         pltpu.make_async_copy(dr.at[step], out.at[step], os.at[step]).start()
 
     first_stage(0)
+
+    @pl.when(k < K - 1)
+    def _():
+        rcopy(hist.at[mine], x1.at[mine], hs.at[0], hr.at[0], (k + 1, s, h)).start()
+
 
     @pl.when(k == 0)
     def _():

time: 61.8 us -> 61.3 us (level)
  no operation moved by 1% of the time
where the time goes in v8:
time: 61.3 us; the launch traced here: 61.1 us
  Pallas kernels  59.5 us (97%)
  matrix products  0.92 us (2%)
  between operations  0.68 us (1%)
    pallas_call x1, Pallas kernels, shards(): pl.pallas_call(functools.partial(kernel, K, Y), out_shape=jax.ShapeDtypeS...  59.5 us

profile of v8, /device:TPU:1, one launch (start us, length us, event | category | flops | bytes accessed | tf_op | source)
XLA Modules:
  0.0 61.1 jit_solution(3964518256983228243)
XLA Ops:
  0.7 0.0 copy-start
  0.7 59.5 %march.1 = bf16[2,4,128,128]{3,2,1,0:T(8,128)(2,1)S(1)} custom-call(s32[2,32]{1,0:T(2,128)} %bitcast.20, s32[1]{0:T(128)} %bitcast.14.used, bf16[32,128,128]{2,1,0:T(8,128)(2,1)} %bitcast.15, bf16[8,128,128]{2,1,0:T(8,128)(2,1)} %bitcast.18, bf16[2,4,128,128]{3,2,1,0:T(8,128)(2,1)} %bitcast.19, bf16[4,128,128]{2,1,0:T(8,128)(2,1)} %bitcast.16), custom_call_target="tpu_custom_call" | custom-call | tf_op jit(solution)/shard_map/march/pallas_call | solution.py:438
  60.2 0.0 copy-done
  60.2 0.9 %convolution_convert_fusion = bf16[2,4,128,128]{2,3,1,0:T(8,128)(2,1)} fusion(bf16[2,4,128,128]{3,2,1,0:T(8,128)(2,1)S(1)} %march.1, bf16[4,128,128]{2,1,0:T(8,128)(2,1)S(1)} %bitcast.17), kind=kOutput, calls=%fused_computation | convolution fusion | flops 33685504 | bytes 655360 | tf_op jit(solution)/shard_map/nbij,nbjw->nbiw/dot_general | solution.py:452
Async XLA Ops:
  0.7 59.6 %copy-start = (bf16[1,4,128,128]{3,2,1,0:T(8,128)(2,1)S(1)}, bf16[1,4,128,128]{3,2,1,0:T(8,128)(2,1)}, u32[]{:S(2)}) copy-start(bf16[1,4,128,128]{3,2,1,0:T(8,128)(2,1)} %param.11) | copy-start | bytes 393220
